TPU v7x, 32 devices: a whole 2x2x4 slice. The times are simulated.
32 devices in a mesh: seq: 16 (over z, y, core), dp: 2 (over x).
Axes of the slice: x: 2, y: 2, z: 4, core: 2. Of those that a mesh axis runs over, the one named last changes fastest.
Arguments:
- xin: bfloat16 [4096, 4096], P(('dp', 'seq')), parts along dimension 0, may hold values from -6 to 6
- zgate: bfloat16 [4096, 4096], P(('dp', 'seq')), parts along dimension 0, may hold values from -6 to 6
- delta_raw: bfloat16 [4096, 4096], P(('dp', 'seq')), parts along dimension 0, may hold values from -6 to 6
- bmat: float32 [16, 4096], P(None, ('dp', 'seq')), parts along dimension 1, may hold values from -6 to 6
- cmat: float32 [16, 4096], P(None, ('dp', 'seq')), parts along dimension 1, may hold values from -6 to 6
- conv_w: float32 [4, 4096], replicated, may hold values from -3 to 3
- conv_b: float32 [4096], replicated, may hold values from -0.5 to 0.5
- decay_rate: float32 [16, 4096], replicated, may hold values from 0.00048828125 to 3
- dskip: float32 [4096], replicated, may hold values from 0.1 to 1.9
- dt_bias: float32 [4096], replicated, may hold values from -6 to -3
- grad_out: bfloat16 [4096, 4096], P(('dp', 'seq')), parts along dimension 0, may hold values from -6 to 6
Outputs:
- grad_x: bfloat16 [4096, 4096], P(('dp', 'seq')), parts along dimension 0
- grad_z: bfloat16 [4096, 4096], P(('dp', 'seq')), parts along dimension 0
- grad_delta: bfloat16 [4096, 4096], P(('dp', 'seq')), parts along dimension 0
- grad_b: float32 [16, 4096], P(None, ('dp', 'seq')), parts along dimension 1
- grad_c: float32 [16, 4096], P(None, ('dp', 'seq')), parts along dimension 1
- grad_convw: float32 [8, 4096], P('dp'), parts along dimension 0
- grad_convb: float32 [8192], P('dp'), parts along dimension 0
- grad_rate: float32 [32, 4096], P('dp'), parts along dimension 0
- grad_skip: float32 [8192], P('dp'), parts along dimension 0
- grad_dtbias: float32 [8192], P('dp'), parts along dimension 0
There are 2 independent parts, one for each index of `dp`. A program takes and returns all parts, laid end to end along the dimension named above; an argument that names none is the same for every part. Nothing has to cross between parts.
All inputs are finite; a program needn't handle non-finite values.
Results may differ from a plain program's by a relative error of at most 0.001.
Values may be sent and summed in bfloat16 or wider, within the bound.
No kernel may reach another device: no remote copies, remote signals or barrier semaphores. Data moves between devices by JAX's collectives and lax.ppermute only.
A program may use at most 448 MiB of HBM per device.

v0:
```python
import functools
import math

import jax
import jax.numpy as jnp
from jax import lax
from jax.experimental import pallas as pl
from jax.experimental.pallas import tpu as pltpu
from jax.sharding import PartitionSpec as P

LANE = 128
SUB = 8
LOG2E = math.log2(math.e)
VMEM_BYTES = 60 * 1024 * 1024


def tile_rows(start):
    return pl.ds(pl.multiple_of(start, SUB), SUB)


def spread(src, dst, blocks, base, scale=None):
    rows = src.shape[0]
    for blk in range(blocks):
        piece = src[:, blk * LANE : (blk + 1) * LANE].astype(jnp.float32)
        if scale is not None:
            piece = piece * scale
        dst[pl.ds(base + blk, rows, stride=blocks), :] = piece


def spread_tokens(src, dst, tokens, blocks, lead):
    def some(group, carry):
        first = pl.multiple_of(group * 16, 16)
        for blk in range(blocks):
            piece = src[pl.ds(first, 16), blk * LANE : (blk + 1) * LANE].astype(jnp.float32)
            dst[pl.ds((first + lead) * blocks + blk, 16, stride=blocks), :] = piece
        return carry

    lax.fori_loop(0, tokens // 16, some, 0)


def gather_tokens(src, dst, tokens, blocks, lead):
    def some(group, carry):
        first = pl.multiple_of(group * 16, 16)
        for blk in range(blocks):
            piece = src[pl.ds((first + lead) * blocks + blk, 16, stride=blocks), :]
            dst[pl.ds(first, 16), blk * LANE : (blk + 1) * LANE] = piece.astype(dst.dtype)
        return carry

    lax.fori_loop(0, tokens // 16, some, 0)


def splat_columns(src, dst, tokens):
    flipped = src[...].T
    for n in range(src.shape[0]):
        dst[pl.ds(n * tokens, tokens), :] = jnp.broadcast_to(flipped[:, n : n + 1], (tokens, LANE))


def splat(ref, row):
    return jnp.broadcast_to(ref[pl.ds(row, 1), :], (SUB, LANE))


def steps(total, unroll, body, carry):
    def several(group, carry):
        for k in range(unroll):
            carry = body(group * unroll + k, carry)
        return carry

    return lax.fori_loop(0, total // unroll, several, carry)


def sigmoid(value):
    return 1.0 / (1.0 + jnp.exp(-value))


def local_body(
    tokens, blocks, nstate, taps,
    x_ref, draw_ref, z_ref, go_ref, rim_ref, b_ref, c_ref, w_ref, cb_ref, dtb_ref, rate_ref,
    pay_ref,
    xs, dts, dus, gys, bs, cs, ws, nrates,
):
    lead = taps - 1
    parts = blocks // SUB
    spread_tokens(x_ref, xs, tokens, blocks, lead)
    xs[0 : lead * blocks, :] = rim_ref[...].astype(jnp.float32)
    spread_tokens(draw_ref, dts, tokens, blocks, 0)
    spread_tokens(z_ref, dus, tokens, blocks, 0)
    spread_tokens(go_ref, gys, tokens, blocks, 0)
    spread(w_ref, ws, blocks, 0)
    spread(rate_ref, nrates, blocks, 0, -LOG2E)
    splat_columns(b_ref, bs, tokens)
    splat_columns(c_ref, cs, tokens)

    for m in range(parts):
        taps_here = [ws[tile_rows(k * blocks + m * SUB), :] for k in range(taps)]
        cb = cb_ref[tile_rows(m * SUB), :]
        dtb = dtb_ref[tile_rows(m * SUB), :]

        def pre(t, total, m=m, taps_here=taps_here, cb=cb, dtb=dtb):
            here = tile_rows(t * blocks + m * SUB)
            conv = cb
            for k in range(taps):
                conv = conv + taps_here[k] * xs[tile_rows((t + k) * blocks + m * SUB), :]
            inner = conv * sigmoid(conv)
            delta = jnp.log1p(jnp.exp(dts[here, :] + dtb))
            zf = dus[here, :]
            gys[here, :] = gys[here, :] * zf * sigmoid(zf)
            dts[here, :] = delta
            dus[here, :] = delta * inner
            return total + delta

        total = steps(tokens, 4, pre, jnp.zeros((SUB, LANE), jnp.float32))
        width = pay_ref.shape[0] // blocks
        pay_ref[pl.ds(m * SUB * width + 2 * nstate, SUB, stride=width), :] = total

    width = pay_ref.shape[0] // blocks
    group = 2
    for first in range(0, nstate, group):
        rates = [
            [nrates[tile_rows((first + n) * blocks + m * SUB), :] for m in range(parts)]
            for n in range(group)
        ]

        def scan(t, carry, first=first, rates=rates):
            state, cum, pulled = carry
            delta = [dts[tile_rows(t * blocks + m * SUB), :] for m in range(parts)]
            driven = [dus[tile_rows(t * blocks + m * SUB), :] for m in range(parts)]
            gy = [gys[tile_rows(t * blocks + m * SUB), :] for m in range(parts)]
            state, cum, pulled = list(state), list(cum), list(pulled)
            for n in range(group):
                bb = splat(bs, (first + n) * tokens + t)
                cc = splat(cs, (first + n) * tokens + t)
                for m in range(parts):
                    at = n * parts + m
                    decay = jnp.exp2(delta[m] * rates[n][m])
                    state[at] = decay * state[at] + driven[m] * bb
                    cum[at] = cum[at] * decay
                    pulled[at] = pulled[at] + cum[at] * (gy[m] * cc)
            return tuple(state), tuple(cum), tuple(pulled)

        zero = jnp.zeros((SUB, LANE), jnp.float32)
        one = jnp.ones((SUB, LANE), jnp.float32)
        count = group * parts
        state, cum, pulled = steps(
            tokens, 4, scan, ((zero,) * count, (one,) * count, (zero,) * count)
        )
        for n in range(group):
            for m in range(parts):
                at = n * parts + m
                pay_ref[pl.ds(m * SUB * width + first + n, SUB, stride=width), :] = state[at]
                pay_ref[pl.ds(m * SUB * width + nstate + first + n, SUB, stride=width), :] = pulled[at]


def carry_body(count, mine, span, nstate, width, got_ref, rate_ref, out_ref):
    for blk in range(mine):
        rate = rate_ref[:, blk * span : (blk + 1) * span]
        state = jnp.zeros((nstate, span), jnp.float32)
        back = jnp.zeros((nstate, span), jnp.float32)
        for step in range(count):
            base, outs = (step * mine + blk) * width, (step * mine + blk) * 2 * nstate
            out_ref[outs : outs + nstate, :] = state
            keep = jnp.exp(-rate * got_ref[base + 2 * nstate : base + 2 * nstate + 1, :])
            state = keep * state + got_ref[base : base + nstate, :]
            run = count - 1 - step
            base, outs = (run * mine + blk) * width, (run * mine + blk) * 2 * nstate
            out_ref[outs + nstate : outs + 2 * nstate, :] = back
            keep = jnp.exp(-rate * got_ref[base + 2 * nstate : base + 2 * nstate + 1, :])
            back = keep * back + got_ref[base + nstate : base + 2 * nstate, :]


def grads_body(
    tokens, blocks, nstate, taps,
    x_ref, draw_ref, z_ref, go_ref, rim_ref, b_ref, c_ref, w_ref, cb_ref, dtb_ref, rate_ref,
    skip_ref, in_ref,
    gx_ref, gz_ref, gd_ref, gb_ref, gc_ref, owed_ref, par_ref,
    xs, dts, dus, us, gys, bs, cs, ws, rates_s, ys, gbs, dds, zfs, sls, hs, pcs, pbs,
):
    lead = taps - 1
    parts = blocks // SUB
    count = 2 * nstate
    spread_tokens(x_ref, xs, tokens, blocks, lead)
    xs[0 : lead * blocks, :] = rim_ref[...].astype(jnp.float32)
    spread_tokens(draw_ref, dts, tokens, blocks, 0)
    spread_tokens(z_ref, zfs, tokens, blocks, 0)
    spread_tokens(go_ref, gys, tokens, blocks, 0)
    spread(w_ref, ws, blocks, 0)
    spread(rate_ref, rates_s, blocks, 0)
    splat_columns(b_ref, bs, tokens)
    splat_columns(c_ref, cs, tokens)
    width = par_ref.shape[0] // blocks
    zero = jnp.zeros((SUB, LANE), jnp.float32)

    for m in range(parts):
        taps_here = [ws[tile_rows(k * blocks + m * SUB), :] for k in range(taps)]
        cb = cb_ref[tile_rows(m * SUB), :]
        dtb = dtb_ref[tile_rows(m * SUB), :]
        skip = skip_ref[tile_rows(m * SUB), :]

        def pre(t, total, m=m, taps_here=taps_here, cb=cb, dtb=dtb, skip=skip):
            here = tile_rows(t * blocks + m * SUB)
            conv = cb
            for k in range(taps):
                conv = conv + taps_here[k] * xs[tile_rows((t + k) * blocks + m * SUB), :]
            sig_c = sigmoid(conv)
            inner = conv * sig_c
            delta = jnp.log1p(jnp.exp(dts[here, :] + dtb))
            zf = zfs[here, :]
            sig_z = sigmoid(zf)
            gof = gys[here, :]
            gy = gof * zf * sig_z
            gys[here, :] = gy
            dts[here, :] = delta
            us[here, :] = inner
            dus[here, :] = delta * inner
            zfs[here, :] = gof * sig_z * (1.0 + zf * (1.0 - sig_z))
            sls[here, :] = sig_c * (1.0 + conv * (1.0 - sig_c))
            ys[here, :] = skip * inner
            gbs[here, :] = zero
            dds[here, :] = zero
            return total + gy * inner

        total = steps(tokens, 4, pre, zero)
        par_ref[pl.ds(m * SUB * width + nstate + taps + 1, SUB, stride=width), :] = total

    group = 4
    cells = group * parts
    for first in range(0, nstate, group):
        def nrate(n, m, first=first):
            return rates_s[tile_rows((first + n) * blocks + m * SUB), :]

        negs = [[-LOG2E * nrate(n, m) for m in range(parts)] for n in range(group)]
        state = tuple(
            in_ref[pl.ds(m * SUB * count + first + n, SUB, stride=count), :]
            for n in range(group)
            for m in range(parts)
        )
        for at in range(cells):
            hs[at * SUB : (at + 1) * SUB, :] = state[at]

        def forward(t, state, first=first, negs=negs):
            delta = [dts[tile_rows(t * blocks + m * SUB), :] for m in range(parts)]
            driven = [dus[tile_rows(t * blocks + m * SUB), :] for m in range(parts)]
            gy = [gys[tile_rows(t * blocks + m * SUB), :] for m in range(parts)]
            y = [ys[tile_rows(t * blocks + m * SUB), :] for m in range(parts)]
            state = list(state)
            for n in range(group):
                bb = splat(bs, (first + n) * tokens + t)
                cc = splat(cs, (first + n) * tokens + t)
                pulled = None
                for m in range(parts):
                    at = n * parts + m
                    decay = jnp.exp2(delta[m] * negs[n][m])
                    now = decay * state[at] + driven[m] * bb
                    state[at] = now
                    hs[tile_rows(((t + 1) * cells + at) * SUB), :] = now
                    y[m] = y[m] + cc * now
                    term = gy[m] * now
                    pulled = term if pulled is None else pulled + term
                pcs[tile_rows((n * tokens + t) * SUB), :] = pulled
            for m in range(parts):
                ys[tile_rows(t * blocks + m * SUB), :] = y[m]
            return tuple(state)

        steps(tokens, 2, forward, state)

        back = tuple(
            in_ref[pl.ds(m * SUB * count + nstate + first + n, SUB, stride=count), :]
            for n in range(group)
            for m in range(parts)
        )

        def backward(step, carry, first=first, nrate=nrate):
            t = tokens - 1 - step
            back, acc = carry
            back, acc = list(back), list(acc)
            delta = [dts[tile_rows(t * blocks + m * SUB), :] for m in range(parts)]
            driven = [dus[tile_rows(t * blocks + m * SUB), :] for m in range(parts)]
            gy = [gys[tile_rows(t * blocks + m * SUB), :] for m in range(parts)]
            gsum = [gbs[tile_rows(t * blocks + m * SUB), :] for m in range(parts)]
            dsum = [dds[tile_rows(t * blocks + m * SUB), :] for m in range(parts)]
            for n in range(group):
                bb = splat(bs, (first + n) * tokens + t)
                cc = splat(cs, (first + n) * tokens + t)
                pulled = None
                for m in range(parts):
                    at = n * parts + m
                    rate = nrate(n, m)
                    scaled = delta[m] * rate
                    decay = jnp.exp2(scaled * -LOG2E)
                    adj = gy[m] * cc + back[at]
                    gsum[m] = gsum[m] + adj * bb
                    pushed = decay * adj
                    back[at] = pushed
                    gah = pushed * hs[tile_rows((t * cells + at) * SUB), :]
                    dsum[m] = dsum[m] + gah * rate
                    acc[at] = acc[at] - gah * delta[m]
                    term = adj * driven[m]
                    pulled = term if pulled is None else pulled + term
                pbs[tile_rows((n * tokens + t) * SUB), :] = pulled
            for m in range(parts):
                gbs[tile_rows(t * blocks + m * SUB), :] = gsum[m]
                dds[tile_rows(t * blocks + m * SUB), :] = dsum[m]
            return tuple(back), tuple(acc)

        _, acc = steps(tokens, 2, backward, (back, (zero,) * cells))
        for n in range(group):
            for m in range(parts):
                at = n * parts + m
                par_ref[pl.ds(m * SUB * width + first + n, SUB, stride=width), :] = acc[at]

        ones = jnp.ones((SUB, LANE), jnp.float32)
        for sums, out in ((pcs, gc_ref), (pbs, gb_ref)):
            for n in range(group):
                rows = sums[pl.ds(n * tokens * SUB, tokens, stride=SUB), :]
                for s in range(1, SUB):
                    rows = rows + sums[pl.ds(n * tokens * SUB + s, tokens, stride=SUB), :]
                line = lax.dot_general(
                    ones, rows, (((1,), (1,)), ((), ())),
                    precision=lax.Precision.HIGHEST, preferred_element_type=jnp.float32,
                )
                out[first + n : first + n + 1, :] = line[0:1, :]

    for m in range(parts):
        dtb = dtb_ref[tile_rows(m * SUB), :]
        skip = skip_ref[tile_rows(m * SUB), :]

        def post(t, carry, m=m, dtb=dtb, skip=skip):
            bias, convb, convw = carry
            here = tile_rows(t * blocks + m * SUB)
            delta, inner, gy = dts[here, :], us[here, :], gys[here, :]
            gsum = gbs[here, :]
            ddt = gsum * inner - dds[here, :]
            dd = ddt * dus[here, :]
            dcv = (gsum * delta + gy * skip) * sls[here, :]
            dds[here, :] = dd
            gbs[here, :] = dcv
            zfs[here, :] = zfs[here, :] * ys[here, :]
            convw = tuple(
                convw[k] + dcv * xs[tile_rows((t + k) * blocks + m * SUB), :] for k in range(taps)
            )
            return bias + dd, convb + dcv, convw

        def refill(t, carry, m=m, dtb=dtb):
            here = tile_rows(t * blocks + m * SUB)
            grow = jnp.exp(dus[here, :] + dtb)
            dus[here, :] = grow / (1.0 + grow)
            return carry

        if m == 0:
            spread_tokens(draw_ref, dus, tokens, blocks, 0)
        steps(tokens, 4, refill, 0)
        bias, convb, convw = steps(tokens, 2, post, (zero, zero, (zero,) * taps))
        for row, value in zip(
            [nstate + k for k in range(taps)] + [nstate + taps, nstate + taps + 2],
            list(convw) + [convb, bias],
        ):
            par_ref[pl.ds(m * SUB * width + row, SUB, stride=width), :] = value
        taps_here = [ws[tile_rows(k * blocks + m * SUB), :] for k in range(taps)]

        def spill(t, carry, m=m, taps_here=taps_here):
            value = taps_here[0] * gbs[tile_rows((t + lead) * blocks + m * SUB), :]
            for k in range(1, taps):
                value = value + taps_here[k] * gbs[tile_rows((t + lead - k) * blocks + m * SUB), :]
            ys[tile_rows(t * blocks + m * SUB), :] = value
            return carry

        lax.fori_loop(0, tokens - lead, spill, 0)
        for s in range(tokens - lead, tokens):
            value = zero
            for k in range(taps):
                if s + lead - k < tokens:
                    value = value + taps_here[k] * gbs[tile_rows((s + lead - k) * blocks + m * SUB), :]
            ys[tile_rows(s * blocks + m * SUB), :] = value
            owed_ref[tile_rows((s - tokens + lead + lead) * blocks + m * SUB), :] = value
        for s in range(lead):
            value = zero
            for k in range(taps):
                if s - k >= 0:
                    value = value + taps_here[k] * gbs[tile_rows((s - k) * blocks + m * SUB), :]
            owed_ref[tile_rows(s * blocks + m * SUB), :] = value

    gather_tokens(ys, gx_ref, tokens, blocks, 0)
    gather_tokens(zfs, gz_ref, tokens, blocks, 0)
    gather_tokens(dds, gd_ref, tokens, blocks, 0)


def whole(count):
    return [pl.BlockSpec(memory_space=pltpu.VMEM)] * count


def slices(rows, runs):
    blocks, width, lanes = rows.shape
    if blocks % runs == 0:
        return rows.reshape(runs, blocks // runs * width, lanes)
    narrow = blocks * lanes // runs
    return rows.transpose(1, 0, 2).reshape(width, runs, narrow).transpose(1, 0, 2)


def unslices(pieces, blocks, width):
    runs = pieces.shape[0]
    if blocks % runs == 0:
        return pieces.reshape(blocks, width, LANE)
    return pieces.transpose(1, 0, 2).reshape(width, blocks, LANE).transpose(1, 0, 2)


def swap(pieces):
    return lax.all_to_all(pieces, "seq", 0, 0, tiled=True)


def shards(xin, zgate, delta_raw, bmat, cmat, conv_w, conv_b, decay_rate, dskip, dt_bias, grad_out):
    tokens, channels = xin.shape
    nstate, taps = bmat.shape[0], conv_w.shape[0]
    lead = taps - 1
    blocks = channels // LANE
    runs = lax.axis_size("seq")
    me = lax.axis_index("seq")
    mine = max(1, blocks // runs)
    span = channels // runs // mine
    vec = lambda rows: pltpu.VMEM((rows, LANE), jnp.float32)
    f32 = lambda *shape: jax.ShapeDtypeStruct(shape, jnp.float32)
    params = pltpu.CompilerParams(vmem_limit_bytes=VMEM_BYTES)

    rim = lax.ppermute(
        xin[tokens - lead :].reshape(lead * blocks, LANE), "seq",
        [(i, i + 1) for i in range(runs - 1)],
    )
    cb, dtb, skip = (v.reshape(blocks, LANE) for v in (conv_b, dt_bias, dskip))
    full = tokens * blocks
    width = 2 * nstate + SUB
    pay = pl.pallas_call(
        functools.partial(local_body, tokens, blocks, nstate, taps),
        out_shape=f32(blocks * width, LANE),
        in_specs=whole(11),
        out_specs=whole(1)[0],
        scratch_shapes=[
            vec(full + lead * blocks), vec(full), vec(full), vec(full),
            vec(nstate * tokens), vec(nstate * tokens), vec(taps * blocks), vec(nstate * blocks),
        ],
        compiler_params=params,
        name="local_scan",
    )(xin, delta_raw, zgate, grad_out, rim, bmat, cmat, conv_w, cb, dtb, decay_rate)
    got = swap(slices(pay.reshape(blocks, width, LANE), runs))
    rate_mine = lax.dynamic_slice(decay_rate, (0, me * mine * span), (nstate, mine * span))
    carries = pl.pallas_call(
        functools.partial(carry_body, runs, mine, span, nstate, width),
        out_shape=f32(runs * mine * 2 * nstate, span),
        in_specs=whole(2),
        out_specs=whole(1)[0],
        compiler_params=params,
        name="carry_scan",
    )(got.reshape(runs * mine * width, span), rate_mine)
    ins = unslices(swap(carries.reshape(runs, mine * 2 * nstate, span)), blocks, 2 * nstate)
    rows = nstate + taps + 4
    rows = rows + (-rows) % SUB
    bf = lambda *shape: jax.ShapeDtypeStruct(shape, jnp.bfloat16)
    gx, gz, gd, gb, gc, owed, par = pl.pallas_call(
        functools.partial(grads_body, tokens, blocks, nstate, taps),
        out_shape=(
            bf(tokens, channels), bf(tokens, channels), bf(tokens, channels),
            f32(nstate, tokens), f32(nstate, tokens),
            f32(2 * lead * blocks, LANE), f32(blocks * rows, LANE),
        ),
        in_specs=whole(13),
        out_specs=tuple(whole(7)),
        scratch_shapes=[
            vec(full + lead * blocks), vec(full), vec(full), vec(full), vec(full),
            vec(nstate * tokens), vec(nstate * tokens), vec(taps * blocks), vec(nstate * blocks),
            vec(full), vec(full), vec(full), vec(full), vec(full),
            vec((tokens + 1) * 4 * blocks), vec(4 * tokens * SUB), vec(4 * tokens * SUB),
        ],
        compiler_params=params,
        name="grads",
    )(xin, delta_raw, zgate, grad_out, rim, bmat, cmat, conv_w, cb, dtb, decay_rate, skip,
      ins.reshape(blocks * 2 * nstate, LANE))
    returned = lax.ppermute(
        owed[: lead * blocks], "seq", [(i + 1, i) for i in range(runs - 1)]
    )
    last = (owed[lead * blocks :] + returned).reshape(lead, channels).astype(jnp.bfloat16)
    gx = lax.dynamic_update_slice(gx, last, (tokens - lead, 0))
    sums = jnp.sum(swap(slices(par.reshape(blocks, rows, LANE), runs)), axis=0)
    every = unslices(swap(jnp.broadcast_to(sums[None], (runs,) + sums.shape)), blocks, rows)
    flat = lambda a, b: every[:, a:b].transpose(1, 0, 2).reshape(b - a, channels)
    return (
        gx, gz, gd, gb, gc,
        flat(nstate, nstate + taps),
        every[:, nstate + taps].reshape(channels),
        flat(0, nstate),
        every[:, nstate + taps + 1].reshape(channels),
        every[:, nstate + taps + 2].reshape(channels),
    )


def solution(mesh):
    both = P(("dp", "seq"), None)
    across = P(None, ("dp", "seq"))
    return jax.shard_map(
        shards,
        mesh=mesh,
        in_specs=(both, both, both, across, across, P(), P(), P(), P(), P(), both),
        out_specs=(
            both, both, both, across, across,
            P("dp", None), P("dp"), P("dp", None), P("dp"), P("dp"),
        ),
        check_vma=False,
    )
```

profile of v0, /device:TPU:0, one launch (start us, length us, event | category | flops | bytes accessed | tf_op | source)
XLA Modules:
  0.0 183.7 jit_solution(2597475543353807739)
XLA Ops:
  0.6 0.9 slice.24
  1.6 2.4 %collective-permute-start = (bf16[96,128]{1,0:T(8,128)(2,1)S(1)}, bf16[96,128]{1,0:T(8,128)(2,1)S(1)}, u32[]{:S(2)}, u32[]{:S(2)}) collective-permute-start(bf16[96,128]{1,0:T(8,128)(2,1)S(1)} %reshape.50), channel_id=1, source_target_pairs={{0,2},{2,4},{4,6},{6,8},{8,10},{10,12},{12,14},{14,16},{16,18},{18... | collective-permute-start | bytes 73736 | tf_op jit(solution)/shard_map/ppermute | solution.py:422
  3.9 0.8 collective-permute-done.rim_ref
  4.8 0.0 copy-start.1
  4.8 0.6 copy-done.1
  5.4 27.3 %local_scan.1 = f32[1280,128]{1,0:T(8,128)} custom-call(bf16[128,4096]{1,0:T(8,128)(2,1)} %x_ref.3, bf16[128,4096]{1,0:T(8,128)(2,1)} %draw_ref.3, bf16[128,4096]{1,0:T(8,128)(2,1)} %z_ref.3, bf16[128,4096]{1,0:T(8,128)(2,1)} %go_ref.3, bf16[96,128]{1,0:T(8,128)(2,1)} %copy-done.1, f32[16,128]{1,0:T(8,128)} %b_ref.3, f32[16,128]{1,0:T(8,128)} %c_ref.3, ...), custom_call_target="tpu_custom_call" | custom-call | tf_op jit(solution)/shard_map/local_scan/pallas_call | solution.py:429
  32.7 9.3 %all-to-all-start = ((f32[16,80,128]{2,1,0:T(8,128)}), f32[16,80,128]{2,1,0:T(8,128)S(1)}, u32[]{:S(2)}, u32[]{:S(2)}) async-start(f32[16,80,128]{2,1,0:T(8,128)} %bitcast.22), calls=%async_computation | async-start | bytes 1310720 | tf_op jit(solution)/shard_map/all_to_all | solution.py:406
  42.1 1.3 constant_dynamic-slice_fusion.rate_ref
  43.4 15.3 %all-to-all-done = f32[16,80,128]{2,1,0:T(8,128)S(1)} async-done(((f32[16,80,128]{2,1,0:T(8,128)}), f32[16,80,128]{2,1,0:T(8,128)S(1)}, u32[]{:S(2)}, u32[]{:S(2)}) %all-to-all-start) | async-done | bytes 655392 | tf_op jit(solution)/shard_map/all_to_all | solution.py:406
  58.7 0.0 copy-start
  58.7 0.8 copy-done
  59.5 2.0 %carry_scan.1 = f32[1024,128]{1,0:T(8,128)} custom-call(f32[1280,128]{1,0:T(8,128)} %bitcast.23, f32[16,256]{1,0:T(8,128)} %constant_dynamic-slice_fusion.rate_ref), custom_call_target="tpu_custom_call" | custom-call | tf_op jit(solution)/shard_map/carry_scan/pallas_call | solution.py:443
  61.4 19.3 %all_to_all.20 = f32[16,64,128]{2,1,0:T(8,128)} all-to-all(f32[16,64,128]{2,1,0:T(8,128)} %bitcast.25), channel_id=1, replica_groups=mesh['seq'=16,'dp'=2] {'seq'}, dimensions={0} | all-to-all | bytes 1048576 | tf_op jit(solution)/shard_map/all_to_all | solution.py:406
  80.8 67.9 %grads.1 = (bf16[128,4096]{1,0:T(8,128)(2,1)}, bf16[128,4096]{1,0:T(8,128)(2,1)}, bf16[128,4096]{1,0:T(8,128)(2,1)}, f32[16,128]{1,0:T(8,128)}, f32[16,128]{1,0:...) custom-call(bf16[128,4096]{1,0:T(8,128)(2,1)} %x_ref.3, bf16[128,4096]{1,0:T(8,128)(2,1)} %draw_ref.3, ...), custom_call_target="tpu_custom_call" | custom-call | tf_op jit(solution)/shard_map/grads/pallas_call | solution.py:455
  148.7 16.3 %all_to_all.21 = f32[16,48,128]{2,1,0:T(8,128)S(1)} all-to-all(f32[16,48,128]{2,1,0:T(8,128)} %bitcast.29), channel_id=1, replica_groups=mesh['seq'=16,'dp'=2] {'seq'}, dimensions={0} | all-to-all | bytes 786432 | tf_op jit(solution)/shard_map/all_to_all | solution.py:406
  165.1 0.8 broadcast_in_dim.2
  165.8 0.0 copy-start.2
  165.8 3.7 %all-to-all-start.3 = ((f32[16,48,128]{2,1,0:T(8,128)}), f32[16,48,128]{2,1,0:T(8,128)S(1)}, u32[]{:S(2)}, u32[]{:S(2)}) async-start(f32[16,48,128]{2,1,0:T(8,128)} %broadcast_in_dim.2), calls=%async_computation.3 | async-start | bytes 786432 | tf_op jit(solution)/shard_map/all_to_all | solution.py:406
  169.5 0.0 copy-done.2
  169.5 1.3 collective-permute-start.1
  170.8 1.8 collective-permute-done.1
  172.7 1.5 dynamic_update_slice.3
  174.2 7.5 %all-to-all-done.3 = f32[16,48,128]{2,1,0:T(8,128)S(1)} async-done(((f32[16,48,128]{2,1,0:T(8,128)}), f32[16,48,128]{2,1,0:T(8,128)S(1)}, u32[]{:S(2)}, u32[]{:S(2)}) %all-to-all-start.3) | async-done | bytes 393248 | tf_op jit(solution)/shard_map/all_to_all | solution.py:406
  181.7 0.6 fusion
  182.3 0.6 slice_bitcast_fusion.1
  183.0 0.7 copy_bitcast_fusion
  (5 shorter events, 0.1 us)
Async XLA Ops:
  1.6 3.2 %collective-permute-start = (bf16[96,128]{1,0:T(8,128)(2,1)S(1)}, bf16[96,128]{1,0:T(8,128)(2,1)S(1)}, u32[]{:S(2)}, u32[]{:S(2)}) collective-permute-start(bf16[96,128]{1,0:T(8,128)(2,1)S(1)} %reshape.50), channel_id=1, source_target_pairs={{0,2},{2,4},{4,6},{6,8},{8,10},{10,12},{12,14},{14,16},{16,18},{18... | collective-permute-start | bytes 73736 | tf_op jit(solution)/shard_map/ppermute | solution.py:422
  4.8 0.6 copy-start.1
  32.7 25.9 %all-to-all-start = ((f32[16,80,128]{2,1,0:T(8,128)}), f32[16,80,128]{2,1,0:T(8,128)S(1)}, u32[]{:S(2)}, u32[]{:S(2)}) async-start(f32[16,80,128]{2,1,0:T(8,128)} %bitcast.22), calls=%async_computation | async-start | bytes 1310720 | tf_op jit(solution)/shard_map/all_to_all | solution.py:406
  58.7 0.8 copy-start
  165.8 3.7 %copy-start.2 = (f32[192,128]{1,0:T(8,128)S(1)}, f32[192,128]{1,0:T(8,128)}, u32[]{:S(2)}) copy-start(f32[192,128]{1,0:T(8,128)} %get-tuple-element.18) | copy-start | bytes 294916
  165.8 15.9 %all-to-all-start.3 = ((f32[16,48,128]{2,1,0:T(8,128)}), f32[16,48,128]{2,1,0:T(8,128)S(1)}, u32[]{:S(2)}, u32[]{:S(2)}) async-start(f32[16,48,128]{2,1,0:T(8,128)} %broadcast_in_dim.2), calls=%async_computation.3 | async-start | bytes 786432 | tf_op jit(solution)/shard_map/all_to_all | solution.py:406
  169.5 3.1 %collective-permute-start.1 = (f32[96,128]{1,0:T(8,128)S(1)}, f32[96,128]{1,0:T(8,128)S(1)}, u32[]{:S(2)}, u32[]{:S(2)}) collective-permute-start(f32[96,128]{1,0:T(8,128)S(1)} %slice.26), channel_id=1, source_target_pairs={{2,0},{4,2},{6,4},{8,6},{10,8},{12,10},{14,12},{16,14},{18,16},{20... | collective-permute-start | bytes 147464 | tf_op jit(solution)/shard_map/ppermute | solution.py:474
where the time goes:
time: 184 us
  Pallas kernels  97.2 us (53%)
  blocking collectives  35.6 us (19%)
  waiting for transfers between devices  25.4 us (14%)
  starting transfers between devices  16.7 us (9%)
  local copies, waits for them, and re-layouts  8.01 us (4%)
    pallas_call x1, Pallas kernels, shards(): pl.pallas_call(functools.partial(grads_body, tokens, blocks, nstate, taps...  67.9 us
    all_to_all x2, blocking collectives, swap(): return lax.all_to_all(pieces, 'seq', 0, 0, tiled=True)  35.6 us
    pallas_call x1, Pallas kernels, shards(): pl.pallas_call(functools.partial(local_body, tokens, blocks, nstate, taps...  27.3 us
    all_to_all x2, waiting for transfers between devices, swap(): return lax.all_to_all(pieces, 'seq', 0, 0, tiled=True)  22.7 us
    all_to_all x2, starting transfers between devices, swap(): return lax.all_to_all(pieces, 'seq', 0, 0, tiled=True)  13 us
  transfers between devices with their start and end apart: 4, of which 4 were waited for; matrix products, arithmetic and copies ran while one was open for 2% of the time, Pallas kernels for 0%

commit v1 on v0

v1 whole, which is shorter than its diff:
```python
import functools
import math

import jax
import jax.numpy as jnp
from jax import lax
from jax.experimental import pallas as pl
from jax.experimental.pallas import tpu as pltpu
from jax.sharding import PartitionSpec as P

LANE = 128
SUB = 8
LOG2E = math.log2(math.e)
VMEM_BYTES = 60 * 1024 * 1024


def tile(start):
    return pl.ds(pl.multiple_of(start, SUB), SUB)


def spread_rows(src, dst, scale=None):
    rows, channels = src.shape
    blocks = channels // LANE
    for blk in range(blocks):
        piece = src[:, blk * LANE : (blk + 1) * LANE]
        dst[pl.ds(blk, rows, stride=blocks), :] = piece if scale is None else piece * scale


def spread_tokens(src, dst, lead=0):
    tokens, channels = src.shape
    blocks = channels // LANE
    plane = dst.shape[0] // (blocks // SUB)

    def some(group, carry):
        first = pl.multiple_of(group * 16, 16)
        for blk in range(blocks):
            piece = src[pl.ds(first, 16), blk * LANE : (blk + 1) * LANE].astype(jnp.float32)
            start = blk // SUB * plane + blk % SUB + (first + lead) * SUB
            dst[pl.ds(start, 16, stride=SUB), :] = piece
        return carry

    lax.fori_loop(0, tokens // 16, some, 0)


def gather_tokens(src, dst):
    tokens, channels = dst.shape
    blocks = channels // LANE
    plane = src.shape[0] // (blocks // SUB)

    def some(group, carry):
        first = pl.multiple_of(group * 16, 16)
        for blk in range(blocks):
            start = blk // SUB * plane + blk % SUB + first * SUB
            piece = src[pl.ds(start, 16, stride=SUB), :]
            dst[pl.ds(first, 16), blk * LANE : (blk + 1) * LANE] = piece.astype(dst.dtype)
        return carry

    lax.fori_loop(0, tokens // 16, some, 0)


def place_rim(rim_ref, xs, lead, parts):
    plane = xs.shape[0] // parts
    for r in range(lead):
        for m in range(parts):
            rows = rim_ref[(r * parts + m) * SUB : (r * parts + m + 1) * SUB, :]
            xs[m * plane + r * SUB : m * plane + (r + 1) * SUB, :] = rows.astype(jnp.float32)


def splat_columns(src, dst, tokens):
    flipped = src[...].T
    for n in range(src.shape[0]):
        dst[pl.ds(n * tokens, tokens), :] = jnp.broadcast_to(flipped[:, n : n + 1], (tokens, LANE))


def splat(ref, row):
    return jnp.broadcast_to(ref[pl.ds(row, 1), :], (SUB, LANE))


def steps(total, unroll, body, carry):
    def several(group, carry):
        for k in range(unroll):
            carry = body(group * unroll + k, carry)
        return carry

    return lax.fori_loop(0, total // unroll, several, carry)


def sigmoid(value):
    return 1.0 / (1.0 + jnp.exp(-value))


def conv_at(xs, ws, cb, m, t, taps, parts):
    plane = xs.shape[0] // parts
    conv = cb
    for k in range(taps):
        conv = conv + ws[k] * xs[tile(m * plane + (t + k) * SUB), :]
    return conv


GROUP = 2


def local_body(
    tokens, blocks, nstate, taps,
    x_ref, draw_ref, z_ref, go_ref, rim_ref, b_ref, c_ref, w_ref, cb_ref, dtb_ref, rate_ref,
    pay_ref,
    xs, dts, dus, gys, bs, cs, ws, nrates,
):
    parts = blocks // SUB
    plane = tokens * SUB
    width = pay_ref.shape[0] // blocks
    spread_tokens(x_ref, xs, taps - 1)
    place_rim(rim_ref, xs, taps - 1, parts)
    spread_tokens(draw_ref, dts)
    spread_tokens(z_ref, dus)
    spread_tokens(go_ref, gys)
    spread_rows(w_ref, ws)
    spread_rows(rate_ref, nrates, -LOG2E)
    splat_columns(b_ref, bs, tokens)
    splat_columns(c_ref, cs, tokens)
    zero = jnp.zeros((SUB, LANE), jnp.float32)
    one = jnp.ones((SUB, LANE), jnp.float32)

    for m in range(parts):
        taps_here = [ws[(k * parts + m) * SUB : (k * parts + m + 1) * SUB, :] for k in range(taps)]
        cb = cb_ref[m * SUB : (m + 1) * SUB, :]
        dtb = dtb_ref[m * SUB : (m + 1) * SUB, :]

        def pre(t, total, m=m, taps_here=taps_here, cb=cb, dtb=dtb):
            here = tile(m * plane + t * SUB)
            conv = conv_at(xs, taps_here, cb, m, t, taps, parts)
            inner = conv * sigmoid(conv)
            delta = jnp.log1p(jnp.exp(dts[here, :] + dtb))
            zf = dus[here, :]
            gys[here, :] = gys[here, :] * zf * sigmoid(zf)
            dts[here, :] = delta
            dus[here, :] = delta * inner
            return total + delta

        total = steps(tokens, 8, pre, zero)
        pay_ref[pl.ds(m * SUB * width + 2 * nstate, SUB, stride=width), :] = total

    def some(group, carry):
        first = group * GROUP
        rates = [
            nrates[tile(((first + n) * parts + m) * SUB), :]
            for n in range(GROUP) for m in range(parts)
        ]

        def scan(t, carry):
            state, cum, pulled = (list(part) for part in carry)
            delta, driven, gy = (
                [ref[tile(m * plane + t * SUB), :] for m in range(parts)] for ref in (dts, dus, gys)
            )
            for n in range(GROUP):
                bb = splat(bs, (first + n) * tokens + t)
                cc = splat(cs, (first + n) * tokens + t)
                for m in range(parts):
                    at = n * parts + m
                    decay = jnp.exp2(delta[m] * rates[at])
                    state[at] = decay * state[at] + driven[m] * bb
                    cum[at] = cum[at] * decay
                    pulled[at] = pulled[at] + cum[at] * (gy[m] * cc)
            return tuple(state), tuple(cum), tuple(pulled)

        count = GROUP * parts
        state, _, pulled = steps(
            tokens, 4, scan, ((zero,) * count, (one,) * count, (zero,) * count)
        )
        for n in range(GROUP):
            for m in range(parts):
                at = n * parts + m
                base = m * SUB * width + first + n
                pay_ref[pl.ds(base, SUB, stride=width), :] = state[at]
                pay_ref[pl.ds(base + nstate, SUB, stride=width), :] = pulled[at]
        return carry

    lax.fori_loop(0, nstate // GROUP, some, 0)


def carry_body(count, mine, span, nstate, width, got_ref, rate_ref, out_ref):
    for blk in range(mine):
        rate = rate_ref[:, blk * span : (blk + 1) * span]
        state = jnp.zeros((nstate, span), jnp.float32)
        back = jnp.zeros((nstate, span), jnp.float32)
        for step in range(count):
            base, outs = (step * mine + blk) * width, (step * mine + blk) * 2 * nstate
            out_ref[outs : outs + nstate, :] = state
            keep = jnp.exp(-rate * got_ref[base + 2 * nstate : base + 2 * nstate + 1, :])
            state = keep * state + got_ref[base : base + nstate, :]
            run = count - 1 - step
            base, outs = (run * mine + blk) * width, (run * mine + blk) * 2 * nstate
            out_ref[outs + nstate : outs + 2 * nstate, :] = back
            keep = jnp.exp(-rate * got_ref[base + 2 * nstate : base + 2 * nstate + 1, :])
            back = keep * back + got_ref[base + nstate : base + 2 * nstate, :]


def grads_body(
    tokens, blocks, nstate, taps,
    x_ref, draw_ref, z_ref, go_ref, rim_ref, b_ref, c_ref, w_ref, cb_ref, dtb_ref, rate_ref,
    skip_ref, in_ref,
    gx_ref, gz_ref, gd_ref, gb_ref, gc_ref, owed_ref, par_ref,
    xs, dts, dus, us, gys, bs, cs, ws, nrates, ys, gbs, dds, zfs, sls, sds, hs, pcs, pbs,
):
    lead = taps - 1
    parts = blocks // SUB
    plane = tokens * SUB
    count = in_ref.shape[0] // blocks
    width = par_ref.shape[0] // blocks
    spread_tokens(x_ref, xs, lead)
    place_rim(rim_ref, xs, lead, parts)
    spread_tokens(draw_ref, dts)
    spread_tokens(z_ref, zfs)
    spread_tokens(go_ref, gys)
    spread_rows(w_ref, ws)
    spread_rows(rate_ref, nrates, -LOG2E)
    splat_columns(b_ref, bs, tokens)
    splat_columns(c_ref, cs, tokens)
    zero = jnp.zeros((SUB, LANE), jnp.float32)

    def taps_of(m):
        return [ws[(k * parts + m) * SUB : (k * parts + m + 1) * SUB, :] for k in range(taps)]

    for m in range(parts):
        taps_here = taps_of(m)
        cb = cb_ref[m * SUB : (m + 1) * SUB, :]
        dtb = dtb_ref[m * SUB : (m + 1) * SUB, :]
        skip = skip_ref[m * SUB : (m + 1) * SUB, :]

        def pre(t, total, m=m, taps_here=taps_here, cb=cb, dtb=dtb, skip=skip):
            here = tile(m * plane + t * SUB)
            conv = conv_at(xs, taps_here, cb, m, t, taps, parts)
            sig_c = sigmoid(conv)
            inner = conv * sig_c
            grow = jnp.exp(dts[here, :] + dtb)
            delta = jnp.log1p(grow)
            zf = zfs[here, :]
            sig_z = sigmoid(zf)
            gof = gys[here, :] * sig_z
            gy = gof * zf
            gys[here, :] = gy
            dts[here, :] = delta
            us[here, :] = inner
            dus[here, :] = delta * inner
            zfs[here, :] = gof * (1.0 + zf * (1.0 - sig_z))
            sls[here, :] = sig_c * (1.0 + conv * (1.0 - sig_c))
            sds[here, :] = grow / (1.0 + grow)
            ys[here, :] = skip * inner
            gbs[here, :] = zero
            dds[here, :] = zero
            return total + gy * inner

        total = steps(tokens, 8, pre, zero)
        par_ref[pl.ds(m * SUB * width + nstate + taps + 1, SUB, stride=width), :] = total

    cells = GROUP * parts

    def some(group, carry):
        first = group * GROUP
        rates = [
            nrates[tile(((first + n) * parts + m) * SUB), :]
            for n in range(GROUP) for m in range(parts)
        ]

        def carried(offset):
            return tuple(
                in_ref[pl.ds(m * SUB * count + offset + first + n, SUB, stride=count), :]
                for n in range(GROUP) for m in range(parts)
            )

        state = carried(0)
        for at in range(cells):
            hs[at * SUB : (at + 1) * SUB, :] = state[at]

        def forward(t, state):
            state = list(state)
            delta, driven, gy, y = (
                [ref[tile(m * plane + t * SUB), :] for m in range(parts)]
                for ref in (dts, dus, gys, ys)
            )
            for n in range(GROUP):
                bb = splat(bs, (first + n) * tokens + t)
                cc = splat(cs, (first + n) * tokens + t)
                pulled = None
                for m in range(parts):
                    at = n * parts + m
                    decay = jnp.exp2(delta[m] * rates[at])
                    now = decay * state[at] + driven[m] * bb
                    state[at] = now
                    hs[tile(((t + 1) * cells + at) * SUB), :] = now
                    y[m] = y[m] + cc * now
                    term = gy[m] * now
                    pulled = term if pulled is None else pulled + term
                pcs[tile((n * tokens + t) * SUB), :] = pulled
            for m in range(parts):
                ys[tile(m * plane + t * SUB), :] = y[m]
            return tuple(state)

        steps(tokens, 4, forward, state)

        def backward(step, carry):
            t = tokens - 1 - step
            back, acc = (list(part) for part in carry)
            delta, driven, gy, gsum, dsum = (
                [ref[tile(m * plane + t * SUB), :] for m in range(parts)]
                for ref in (dts, dus, gys, gbs, dds)
            )
            for n in range(GROUP):
                bb = splat(bs, (first + n) * tokens + t)
                cc = splat(cs, (first + n) * tokens + t)
                pulled = None
                for m in range(parts):
                    at = n * parts + m
                    decay = jnp.exp2(delta[m] * rates[at])
                    adj = gy[m] * cc + back[at]
                    gsum[m] = gsum[m] + adj * bb
                    back[at] = decay * adj
                    gah = back[at] * hs[tile((t * cells + at) * SUB), :]
                    dsum[m] = dsum[m] + gah * rates[at]
                    acc[at] = acc[at] + gah * delta[m]
                    term = adj * driven[m]
                    pulled = term if pulled is None else pulled + term
                pbs[tile((n * tokens + t) * SUB), :] = pulled
            for m in range(parts):
                gbs[tile(m * plane + t * SUB), :] = gsum[m]
                dds[tile(m * plane + t * SUB), :] = dsum[m]
            return tuple(back), tuple(acc)

        _, acc = steps(tokens, 2, backward, (carried(nstate), (zero,) * cells))
        for n in range(GROUP):
            for m in range(parts):
                base = m * SUB * width + first + n
                par_ref[pl.ds(base, SUB, stride=width), :] = -acc[n * parts + m]

        def fold(piece, carry):
            for sums, out in ((pcs, gc_ref), (pbs, gb_ref)):
                rows = sums[pl.ds(piece * 32 * SUB, 32, stride=SUB), :]
                for s in range(1, SUB):
                    rows = rows + sums[pl.ds(piece * 32 * SUB + s, 32, stride=SUB), :]
                out[pl.ds(pl.multiple_of(first * tokens + piece * 32, 32), 32), :] = rows
            return carry

        lax.fori_loop(0, GROUP * tokens // 32, fold, 0)
        return carry

    lax.fori_loop(0, nstate // GROUP, some, 0)

    for m in range(parts):
        taps_here = taps_of(m)
        skip = skip_ref[m * SUB : (m + 1) * SUB, :]
        xplane = xs.shape[0] // parts

        def post(t, carry, m=m, skip=skip):
            bias, convb, convw = carry
            here = tile(m * plane + t * SUB)
            gsum = gbs[here, :]
            dd = (gsum * us[here, :] + dds[here, :] * (1.0 / LOG2E)) * sds[here, :]
            dcv = (gsum * dts[here, :] + gys[here, :] * skip) * sls[here, :]
            dds[here, :] = dd
            gbs[here, :] = dcv
            zfs[here, :] = zfs[here, :] * ys[here, :]
            convw = tuple(
                convw[k] + dcv * xs[tile(m * xplane + (t + k) * SUB), :] for k in range(taps)
            )
            return bias + dd, convb + dcv, convw

        bias, convb, convw = steps(tokens, 4, post, (zero, zero, (zero,) * taps))
        rows = [nstate + k for k in range(taps)] + [nstate + taps, nstate + taps + 2]
        for row, value in zip(rows, list(convw) + [convb, bias]):
            par_ref[pl.ds(m * SUB * width + row, SUB, stride=width), :] = value

        def spill(t, carry, m=m, taps_here=taps_here):
            value = None
            for k in range(taps):
                term = taps_here[k] * gbs[tile(m * plane + (t + lead - k) * SUB), :]
                value = term if value is None else value + term
            ys[tile(m * plane + t * SUB), :] = value
            return carry

        whole_steps = (tokens - lead) // 8 * 8
        steps(whole_steps, 8, spill, 0)
        for t in range(whole_steps, tokens - lead):
            spill(t, 0)

        def partial(s):
            value = zero
            for k in range(taps):
                if 0 <= s + lead - k < tokens:
                    value = value + taps_here[k] * gbs[tile(m * plane + (s + lead - k) * SUB), :]
            return value

        for i in range(lead):
            value = partial(tokens - lead + i)
            ys[tile(m * plane + (tokens - lead + i) * SUB), :] = value
            owed_ref[tile(((lead + i) * parts + m) * SUB), :] = value
            owed_ref[tile((i * parts + m) * SUB), :] = partial(i - lead)

    gather_tokens(ys, gx_ref)
    gather_tokens(zfs, gz_ref)
    gather_tokens(dds, gd_ref)


def whole(count):
    return [pl.BlockSpec(memory_space=pltpu.VMEM)] * count


def slices(rows, runs):
    blocks, width, lanes = rows.shape
    if blocks % runs == 0:
        return rows.reshape(runs, blocks // runs * width, lanes)
    narrow = blocks * lanes // runs
    return rows.transpose(1, 0, 2).reshape(width, runs, narrow).transpose(1, 0, 2)


def unslices(pieces, blocks, width):
    runs = pieces.shape[0]
    if blocks % runs == 0:
        return pieces.reshape(blocks, width, LANE)
    return pieces.transpose(1, 0, 2).reshape(width, blocks, LANE).transpose(1, 0, 2)


def swap(pieces):
    return lax.all_to_all(pieces, "seq", 0, 0, tiled=True)


def shards(xin, zgate, delta_raw, bmat, cmat, conv_w, conv_b, decay_rate, dskip, dt_bias, grad_out):
    tokens, channels = xin.shape
    nstate, taps = bmat.shape[0], conv_w.shape[0]
    lead = taps - 1
    blocks = channels // LANE
    runs = lax.axis_size("seq")
    me = lax.axis_index("seq")
    mine = max(1, blocks // runs)
    span = channels // runs // mine
    vec = lambda rows: pltpu.VMEM((rows, LANE), jnp.float32)
    f32 = lambda *shape: jax.ShapeDtypeStruct(shape, jnp.float32)
    params = pltpu.CompilerParams(vmem_limit_bytes=VMEM_BYTES)

    rim = lax.ppermute(
        xin[tokens - lead :].reshape(lead * blocks, LANE), "seq",
        [(i, i + 1) for i in range(runs - 1)],
    )
    cb, dtb, skip = (v.reshape(blocks, LANE) for v in (conv_b, dt_bias, dskip))
    full = tokens * blocks
    width = 2 * nstate + SUB
    pay = pl.pallas_call(
        functools.partial(local_body, tokens, blocks, nstate, taps),
        out_shape=f32(blocks * width, LANE),
        in_specs=whole(11),
        out_specs=whole(1)[0],
        scratch_shapes=[
            vec(full + lead * blocks), vec(full), vec(full), vec(full),
            vec(nstate * tokens), vec(nstate * tokens), vec(taps * blocks), vec(nstate * blocks),
        ],
        compiler_params=params,
        name="local_scan",
    )(xin, delta_raw, zgate, grad_out, rim, bmat, cmat, conv_w, cb, dtb, decay_rate)
    got = swap(slices(pay.reshape(blocks, width, LANE), runs))
    rate_mine = lax.dynamic_slice(decay_rate, (0, me * mine * span), (nstate, mine * span))
    carries = pl.pallas_call(
        functools.partial(carry_body, runs, mine, span, nstate, width),
        out_shape=f32(runs * mine * 2 * nstate, span),
        in_specs=whole(2),
        out_specs=whole(1)[0],
        compiler_params=params,
        name="carry_scan",
    )(got.reshape(runs * mine * width, span), rate_mine)
    ins = unslices(swap(carries.reshape(runs, mine * 2 * nstate, span)), blocks, 2 * nstate)
    rows = nstate + taps + 4
    rows = rows + (-rows) % SUB
    bf = lambda *shape: jax.ShapeDtypeStruct(shape, jnp.bfloat16)
    gx, gz, gd, gb, gc, owed, par = pl.pallas_call(
        functools.partial(grads_body, tokens, blocks, nstate, taps),
        out_shape=(
            bf(tokens, channels), bf(tokens, channels), bf(tokens, channels),
            f32(nstate * tokens, LANE), f32(nstate * tokens, LANE),
            f32(2 * lead * blocks, LANE), f32(blocks * rows, LANE),
        ),
        in_specs=whole(13),
        out_specs=tuple(whole(7)),
        scratch_shapes=[
            vec(full + lead * blocks), vec(full), vec(full), vec(full), vec(full),
            vec(nstate * tokens), vec(nstate * tokens), vec(taps * blocks), vec(nstate * blocks),
            vec(full), vec(full), vec(full), vec(full), vec(full), vec(full),
            vec((tokens + 1) * GROUP * blocks), vec(GROUP * tokens * SUB), vec(GROUP * tokens * SUB),
        ],
        compiler_params=params,
        name="grads",
    )(xin, delta_raw, zgate, grad_out, rim, bmat, cmat, conv_w, cb, dtb, decay_rate, skip,
      ins.reshape(blocks * 2 * nstate, LANE))
    gb, gc = (jnp.sum(v.reshape(nstate, tokens, LANE), axis=2) for v in (gb, gc))
    returned = lax.ppermute(
        owed[: lead * blocks], "seq", [(i + 1, i) for i in range(runs - 1)]
    )
    last = (owed[lead * blocks :] + returned).reshape(lead, channels).astype(jnp.bfloat16)
    gx = lax.dynamic_update_slice(gx, last, (tokens - lead, 0))
    sums = jnp.sum(swap(slices(par.reshape(blocks, rows, LANE), runs)), axis=0)
    every = unslices(swap(jnp.broadcast_to(sums[None], (runs,) + sums.shape)), blocks, rows)
    flat = lambda a, b: every[:, a:b].transpose(1, 0, 2).reshape(b - a, channels)
    return (
        gx, gz, gd, gb, gc,
        flat(nstate, nstate + taps),
        every[:, nstate + taps].reshape(channels),
        flat(0, nstate),
        every[:, nstate + taps + 1].reshape(channels),
        every[:, nstate + taps + 2].reshape(channels),
    )


def solution(mesh):
    both = P(("dp", "seq"), None)
    across = P(None, ("dp", "seq"))
    return jax.shard_map(
        shards,
        mesh=mesh,
        in_specs=(both, both, both, across, across, P(), P(), P(), P(), P(), both),
        out_specs=(
            both, both, both, across, across,
            P("dp", None), P("dp"), P("dp", None), P("dp"), P("dp"),
        ),
        check_vma=False,
    )
```

time: 184 us -> 162 us (0.88)
  Pallas kernels: 97.2 us -> 75 us
  waiting for transfers between devices: 25.4 us -> 23.5 us
  other arithmetic: 0.04 us -> 1.92 us
    pallas_call x1, Pallas kernels: 67.9 us -> 51.4 us  [shards(): pl.pallas_call(functools.partial(grads_body, tokens, blocks, nstate, taps...]
    pallas_call x1, Pallas kernels: 27.3 us -> 21.6 us  [shards(): pl.pallas_call(functools.partial(local_body, tokens, blocks, nstate, taps...]
    reduce_sum x0 -> x2, other arithmetic: none -> 1.88 us  [shards(): jnp.sum(v.reshape(nstate, tokens, LANE), axis=2)]
  transfers between devices with their start and end apart: 4 -> 4, of which waited for: 4 -> 3; matrix products, arithmetic and copies ran while one was open for 2% -> 3% of each run, Pallas kernels for 0% -> 0%
where the time goes in v1:
time: 162 us; the launch traced here: 161 us
  Pallas kernels  75 us (46%)
  blocking collectives  35.6 us (22%)
  waiting for transfers between devices  23.5 us (15%)
  starting transfers between devices  16.7 us (10%)
  local copies, waits for them, and re-layouts  8.01 us (5%)
  other arithmetic  1.92 us (1%)
    pallas_call x1, Pallas kernels, shards(): pl.pallas_call(functools.partial(grads_body, tokens, blocks, nstate, taps...  51.4 us
    all_to_all x2, blocking collectives, swap(): return lax.all_to_all(pieces, 'seq', 0, 0, tiled=True)  35.6 us
    all_to_all x2, waiting for transfers between devices, swap(): return lax.all_to_all(pieces, 'seq', 0, 0, tiled=True)  22.6 us
    pallas_call x1, Pallas kernels, shards(): pl.pallas_call(functools.partial(local_body, tokens, blocks, nstate, taps...  21.6 us
    all_to_all x2, starting transfers between devices, swap(): return lax.all_to_all(pieces, 'seq', 0, 0, tiled=True)  13 us
  transfers between devices with their start and end apart: 4, of which 3 were waited for; matrix products, arithmetic and copies ran while one was open for 3% of the time, Pallas kernels for 0%

profile of v1, /device:TPU:0, one launch (start us, length us, event | category | flops | bytes accessed | tf_op | source)
XLA Modules:
  0.0 161.4 jit_solution(2901234019518737481)
XLA Ops:
  0.6 0.9 slice.24
  1.6 2.4 %collective-permute-start = (bf16[96,128]{1,0:T(8,128)(2,1)S(1)}, bf16[96,128]{1,0:T(8,128)(2,1)S(1)}, u32[]{:S(2)}, u32[]{:S(2)}) collective-permute-start(bf16[96,128]{1,0:T(8,128)(2,1)S(1)} %reshape.54), channel_id=1, source_target_pairs={{0,2},{2,4},{4,6},{6,8},{8,10},{10,12},{12,14},{14,16},{16,18},{18... | collective-permute-start | bytes 73736 | tf_op jit(solution)/shard_map/ppermute | solution.py:439
  3.9 0.8 collective-permute-done.rim_ref
  4.8 0.0 copy-start.3
  4.8 0.6 copy-done.3
  5.4 21.6 %local_scan.1 = f32[1280,128]{1,0:T(8,128)} custom-call(bf16[128,4096]{1,0:T(8,128)(2,1)} %x_ref.3, bf16[128,4096]{1,0:T(8,128)(2,1)} %draw_ref.3, bf16[128,4096]{1,0:T(8,128)(2,1)} %z_ref.3, bf16[128,4096]{1,0:T(8,128)(2,1)} %go_ref.3, bf16[96,128]{1,0:T(8,128)(2,1)} %copy-done.3, f32[16,128]{1,0:T(8,128)} %b_ref.3, f32[16,128]{1,0:T(8,128)} %c_ref.3, ...), custom_call_target="tpu_custom_call" | custom-call | tf_op jit(solution)/shard_map/local_scan/pallas_call | solution.py:446
  27.0 9.3 %all-to-all-start = ((f32[16,80,128]{2,1,0:T(8,128)}), f32[16,80,128]{2,1,0:T(8,128)S(1)}, u32[]{:S(2)}, u32[]{:S(2)}) async-start(f32[16,80,128]{2,1,0:T(8,128)} %bitcast.24), calls=%async_computation | async-start | bytes 1310720 | tf_op jit(solution)/shard_map/all_to_all | solution.py:423
  36.4 1.3 constant_dynamic-slice_fusion.rate_ref
  37.7 15.3 %all-to-all-done = f32[16,80,128]{2,1,0:T(8,128)S(1)} async-done(((f32[16,80,128]{2,1,0:T(8,128)}), f32[16,80,128]{2,1,0:T(8,128)S(1)}, u32[]{:S(2)}, u32[]{:S(2)}) %all-to-all-start) | async-done | bytes 655392 | tf_op jit(solution)/shard_map/all_to_all | solution.py:423
  53.0 0.0 copy-start
  53.0 0.8 copy-done
  53.8 2.0 %carry_scan.1 = f32[1024,128]{1,0:T(8,128)} custom-call(f32[1280,128]{1,0:T(8,128)} %bitcast.25, f32[16,256]{1,0:T(8,128)} %constant_dynamic-slice_fusion.rate_ref), custom_call_target="tpu_custom_call" | custom-call | tf_op jit(solution)/shard_map/carry_scan/pallas_call | solution.py:460
  55.7 19.3 %all_to_all.20 = f32[16,64,128]{2,1,0:T(8,128)} all-to-all(f32[16,64,128]{2,1,0:T(8,128)} %bitcast.27), channel_id=1, replica_groups=mesh['seq'=16,'dp'=2] {'seq'}, dimensions={0} | all-to-all | bytes 1048576 | tf_op jit(solution)/shard_map/all_to_all | solution.py:423
  75.1 51.4 %grads.1 = (bf16[128,4096]{1,0:T(8,128)(2,1)}, bf16[128,4096]{1,0:T(8,128)(2,1)}, bf16[128,4096]{1,0:T(8,128)(2,1)}, f32[2048,128]{1,0:T(8,128)}, f32[2048,128]{...) custom-call(bf16[128,4096]{1,0:T(8,128)(2,1)} %x_ref.3, bf16[128,4096]{1,0:T(8,128)(2,1)} %draw_ref.3, ...), custom_call_target="tpu_custom_call" | custom-call | tf_op jit(solution)/shard_map/grads/pallas_call | solution.py:472
  126.5 16.3 %all_to_all.21 = f32[16,48,128]{2,1,0:T(8,128)S(1)} all-to-all(f32[16,48,128]{2,1,0:T(8,128)} %bitcast.31), channel_id=1, replica_groups=mesh['seq'=16,'dp'=2] {'seq'}, dimensions={0} | all-to-all | bytes 786432 | tf_op jit(solution)/shard_map/all_to_all | solution.py:423
  142.8 0.0 copy-start.2
  142.8 0.0 copy-start.4
  142.8 0.8 broadcast_in_dim.2
  143.6 0.0 copy-start.1
  143.6 3.7 %all-to-all-start.3 = ((f32[16,48,128]{2,1,0:T(8,128)}), f32[16,48,128]{2,1,0:T(8,128)S(1)}, u32[]{:S(2)}, u32[]{:S(2)}) async-start(f32[16,48,128]{2,1,0:T(8,128)} %broadcast_in_dim.2), calls=%async_computation.3 | async-start | bytes 786432 | tf_op jit(solution)/shard_map/all_to_all | solution.py:423
  147.3 0.0 copy-done.4
  147.3 1.3 collective-permute-start.1
  148.6 0.0 copy-done.2
  148.6 0.9 reduce_sum.31
  149.5 0.0 copy-done.1
  149.5 0.9 reduce_sum.33
  150.5 0.0 collective-permute-done.1
  150.5 1.5 dynamic_update_slice.3
  152.0 7.4 %all-to-all-done.3 = f32[16,48,128]{2,1,0:T(8,128)S(1)} async-done(((f32[16,48,128]{2,1,0:T(8,128)}), f32[16,48,128]{2,1,0:T(8,128)S(1)}, u32[]{:S(2)}, u32[]{:S(2)}) %all-to-all-start.3) | async-done | bytes 393248 | tf_op jit(solution)/shard_map/all_to_all | solution.py:423
  159.4 0.6 fusion
  160.1 0.6 slice_bitcast_fusion.1
  160.7 0.7 copy_bitcast_fusion
  (5 shorter events, 0.1 us)
Async XLA Ops:
  1.6 3.2 %collective-permute-start = (bf16[96,128]{1,0:T(8,128)(2,1)S(1)}, bf16[96,128]{1,0:T(8,128)(2,1)S(1)}, u32[]{:S(2)}, u32[]{:S(2)}) collective-permute-start(bf16[96,128]{1,0:T(8,128)(2,1)S(1)} %reshape.54), channel_id=1, source_target_pairs={{0,2},{2,4},{4,6},{6,8},{8,10},{10,12},{12,14},{14,16},{16,18},{18... | collective-permute-start | bytes 73736 | tf_op jit(solution)/shard_map/ppermute | solution.py:439
  4.8 0.6 copy-start.3
  27.0 25.9 %all-to-all-start = ((f32[16,80,128]{2,1,0:T(8,128)}), f32[16,80,128]{2,1,0:T(8,128)S(1)}, u32[]{:S(2)}, u32[]{:S(2)}) async-start(f32[16,80,128]{2,1,0:T(8,128)} %bitcast.24), calls=%async_computation | async-start | bytes 1310720 | tf_op jit(solution)/shard_map/all_to_all | solution.py:423
  53.0 0.8 copy-start
  142.8 5.8 %copy-start.2 = (f32[2048,128]{1,0:T(8,128)S(1)}, f32[2048,128]{1,0:T(8,128)}, u32[]{:S(2)}) copy-start(f32[2048,128]{1,0:T(8,128)} %get-tuple-element.21) | copy-start | bytes 3145732
  142.8 4.5 %copy-start.4 = (f32[192,128]{1,0:T(8,128)S(1)}, f32[192,128]{1,0:T(8,128)}, u32[]{:S(2)}) copy-start(f32[192,128]{1,0:T(8,128)} %get-tuple-element.18) | copy-start | bytes 294916
  143.6 6.0 %copy-start.1 = (f32[2048,128]{1,0:T(8,128)S(1)}, f32[2048,128]{1,0:T(8,128)}, u32[]{:S(2)}) copy-start(f32[2048,128]{1,0:T(8,128)} %get-tuple-element.22) | copy-start | bytes 3145732
  143.6 15.9 %all-to-all-start.3 = ((f32[16,48,128]{2,1,0:T(8,128)}), f32[16,48,128]{2,1,0:T(8,128)S(1)}, u32[]{:S(2)}, u32[]{:S(2)}) async-start(f32[16,48,128]{2,1,0:T(8,128)} %broadcast_in_dim.2), calls=%async_computation.3 | async-start | bytes 786432 | tf_op jit(solution)/shard_map/all_to_all | solution.py:423
  147.3 3.2 %collective-permute-start.1 = (f32[96,128]{1,0:T(8,128)S(1)}, f32[96,128]{1,0:T(8,128)S(1)}, u32[]{:S(2)}, u32[]{:S(2)}) collective-permute-start(f32[96,128]{1,0:T(8,128)S(1)} %slice.26), channel_id=1, source_target_pairs={{2,0},{4,2},{6,4},{8,6},{10,8},{12,10},{14,12},{16,14},{18,16},{20... | collective-permute-start | bytes 147464 | tf_op jit(solution)/shard_map/ppermute | solution.py:492

commit v2 on v1

v2 whole, which is shorter than its diff:
```python
import functools
import math

import jax
import jax.numpy as jnp
from jax import lax
from jax.experimental import pallas as pl
from jax.experimental.pallas import tpu as pltpu
from jax.sharding import PartitionSpec as P

LANE = 128
SUB = 8
LOG2E = math.log2(math.e)
LOCAL_MB, CARRY_MB, GRADS_MB = 20, 2, 30


def tile(start):
    return pl.ds(pl.multiple_of(start, SUB), SUB)


def spread_rows(src, dst, scale=None):
    rows, channels = src.shape
    blocks = channels // LANE
    for blk in range(blocks):
        piece = src[:, blk * LANE : (blk + 1) * LANE]
        dst[pl.ds(blk, rows, stride=blocks), :] = piece if scale is None else piece * scale


def spread_tokens(src, dst, lead=0):
    tokens, channels = src.shape
    blocks = channels // LANE
    plane = dst.shape[0] // (blocks // SUB)

    def some(group, carry):
        first = pl.multiple_of(group * 16, 16)
        for blk in range(blocks):
            piece = src[pl.ds(first, 16), blk * LANE : (blk + 1) * LANE].astype(jnp.float32)
            start = blk // SUB * plane + blk % SUB + (first + lead) * SUB
            dst[pl.ds(start, 16, stride=SUB), :] = piece
        return carry

    lax.fori_loop(0, tokens // 16, some, 0)


def gather_tokens(src, dst):
    tokens, channels = dst.shape
    blocks = channels // LANE
    plane = src.shape[0] // (blocks // SUB)

    def some(group, carry):
        first = pl.multiple_of(group * 16, 16)
        for blk in range(blocks):
            start = blk // SUB * plane + blk % SUB + first * SUB
            piece = src[pl.ds(start, 16, stride=SUB), :]
            dst[pl.ds(first, 16), blk * LANE : (blk + 1) * LANE] = piece.astype(dst.dtype)
        return carry

    lax.fori_loop(0, tokens // 16, some, 0)


def place_rim(rim_ref, xs, lead, parts):
    plane = xs.shape[0] // parts
    for r in range(lead):
        for m in range(parts):
            rows = rim_ref[r, m * SUB : (m + 1) * SUB, :]
            xs[m * plane + r * SUB : m * plane + (r + 1) * SUB, :] = rows.astype(jnp.float32)


def splat_columns(src, dst, tokens):
    flipped = src[...].T
    for n in range(src.shape[0]):
        dst[pl.ds(n * tokens, tokens), :] = jnp.broadcast_to(flipped[:, n : n + 1], (tokens, LANE))


def splat(ref, row):
    return jnp.broadcast_to(ref[pl.ds(row, 1), :], (SUB, LANE))


def steps(total, unroll, body, carry):
    def several(group, carry):
        for k in range(unroll):
            carry = body(group * unroll + k, carry)
        return carry

    return lax.fori_loop(0, total // unroll, several, carry)


def sigmoid(value):
    return 1.0 / (1.0 + jnp.exp(-value))


def conv_at(xs, ws, cb, m, t, taps, parts):
    plane = xs.shape[0] // parts
    conv = cb
    for k in range(taps):
        conv = conv + ws[k] * xs[tile(m * plane + (t + k) * SUB), :]
    return conv


GROUP = 2


def rows_at(refs, t, parts, plane):
    return [[ref[tile(m * plane + t * SUB), :] for m in range(parts)] for ref in refs]


def rates_at(nrates, first, group, parts):
    return [
        nrates[tile(((first + n) * parts + m) * SUB), :] for n in range(group) for m in range(parts)
    ]


def local_body(
    tokens, blocks, nstate, taps,
    x_hbm, draw_hbm, z_hbm, go_hbm, rim_ref, b_ref, c_ref, w_ref, cb_ref, dtb_ref, rate_ref,
    rate_mine_ref,
    pay_ref, skip_ref, dts, dus, gys, us, zfs, sls, sds, xs, bs, cs, nrates,
    ws, raw, sems,
):
    lead = taps - 1
    parts = blocks // SUB
    plane = tokens * SUB
    width = pay_ref.shape[0] // blocks
    copies = [
        pltpu.make_async_copy(src, raw.at[i], sems.at[i])
        for i, src in enumerate((draw_hbm, z_hbm, go_hbm, x_hbm))
    ]
    for copy in copies:
        copy.start()
    spread_rows(w_ref, ws)
    spread_rows(rate_ref, nrates, -LOG2E)
    splat_columns(b_ref, bs, tokens)
    splat_columns(c_ref, cs, tokens)
    place_rim(rim_ref, xs, lead, parts)
    for i, (dst, ahead) in enumerate(((dts, 0), (zfs, 0), (gys, 0), (xs, lead))):
        copies[i].wait()
        spread_tokens(raw.at[i], dst, ahead)
    zero = jnp.zeros((SUB, LANE), jnp.float32)

    for m in range(parts):
        taps_here = [ws[(k * parts + m) * SUB : (k * parts + m + 1) * SUB, :] for k in range(taps)]
        cb = cb_ref[m * SUB : (m + 1) * SUB, :]
        dtb = dtb_ref[m * SUB : (m + 1) * SUB, :]

        def pre(t, totals, m=m, taps_here=taps_here, cb=cb, dtb=dtb):
            here = tile(m * plane + t * SUB)
            conv = conv_at(xs, taps_here, cb, m, t, taps, parts)
            sig_c = sigmoid(conv)
            inner = conv * sig_c
            grow = jnp.exp(dts[here, :] + dtb)
            delta = jnp.log1p(grow)
            zf = zfs[here, :]
            sig_z = sigmoid(zf)
            gof = gys[here, :] * sig_z
            gy = gof * zf
            gys[here, :] = gy
            dts[here, :] = delta
            us[here, :] = inner
            dus[here, :] = delta * inner
            zfs[here, :] = gof * (1.0 + zf * (1.0 - sig_z))
            sls[here, :] = sig_c * (1.0 + conv * (1.0 - sig_c))
            sds[here, :] = grow / (1.0 + grow)
            return totals[0] + delta, totals[1] + gy * inner

        total, skipped = steps(tokens, 8, pre, (zero, zero))
        pay_ref[pl.ds(m * SUB * width + 2 * nstate, SUB, stride=width), :] = total
        skip_ref[m * SUB : (m + 1) * SUB, :] = skipped

    one = jnp.ones((SUB, LANE), jnp.float32)

    def some(group, carry):
        first = group * GROUP
        rates = rates_at(nrates, first, GROUP, parts)

        def scan(t, carry):
            state, cum, pulled = (list(part) for part in carry)
            delta, driven, gy = rows_at((dts, dus, gys), t, parts, plane)
            for n in range(GROUP):
                bb = splat(bs, (first + n) * tokens + t)
                cc = splat(cs, (first + n) * tokens + t)
                for m in range(parts):
                    at = n * parts + m
                    decay = jnp.exp2(delta[m] * rates[at])
                    state[at] = decay * state[at] + driven[m] * bb
                    cum[at] = cum[at] * decay
                    pulled[at] = pulled[at] + cum[at] * (gy[m] * cc)
            return tuple(state), tuple(cum), tuple(pulled)

        count = GROUP * parts
        state, _, pulled = steps(
            tokens, 32, scan, ((zero,) * count, (one,) * count, (zero,) * count)
        )
        for n in range(GROUP):
            for m in range(parts):
                at = n * parts + m
                base = m * SUB * width + first + n
                pay_ref[pl.ds(base, SUB, stride=width), :] = state[at]
                pay_ref[pl.ds(base + nstate, SUB, stride=width), :] = pulled[at]
        return carry

    lax.fori_loop(0, nstate // GROUP, some, 0)


def carry_body(count, mine, span, nstate, width, got_ref, rate_ref, out_ref):
    for blk in range(mine):
        rate = rate_ref[:, blk * span : (blk + 1) * span]
        state = jnp.zeros((nstate, span), jnp.float32)
        back = jnp.zeros((nstate, span), jnp.float32)
        for step in range(count):
            base, outs = (step * mine + blk) * width, (step * mine + blk) * 2 * nstate
            out_ref[outs : outs + nstate, :] = state
            keep = jnp.exp(-rate * got_ref[base + 2 * nstate : base + 2 * nstate + 1, :])
            state = keep * state + got_ref[base : base + nstate, :]
            run = count - 1 - step
            base, outs = (run * mine + blk) * width, (run * mine + blk) * 2 * nstate
            out_ref[outs + nstate : outs + 2 * nstate, :] = back
            keep = jnp.exp(-rate * got_ref[base + 2 * nstate : base + 2 * nstate + 1, :])
            back = keep * back + got_ref[base + nstate : base + 2 * nstate, :]


def fold(sums, out, base, count):
    def some(piece, carry):
        rows = sums[pl.ds(piece * 64 * SUB, 64, stride=SUB), :]
        for s in range(1, SUB):
            rows = rows + sums[pl.ds(piece * 64 * SUB + s, 64, stride=SUB), :]
        out[pl.ds(pl.multiple_of(base + piece * 64, 64), 64), :] = rows
        return carry

    lax.fori_loop(0, count // 64, some, 0)


def grads_body(
    tokens, blocks, nstate, taps,
    in_ref, w_ref, skip_ref, skipped_ref, dts, dus, gys, us, zfs, sls, sds, xs, bs, cs, nrates,
    gx_ref, gz_ref, gd_ref, gb_ref, gc_ref, owed_ref, par_ref,
    ys, gbs, dds, hs, pcs, pbs, ws,
):
    lead = taps - 1
    parts = blocks // SUB
    plane = tokens * SUB
    count = in_ref.shape[0] // blocks
    width = par_ref.shape[0] // blocks
    zero = jnp.zeros((SUB, LANE), jnp.float32)
    spread_rows(w_ref, ws)

    def clear(t, carry):
        for m in range(parts):
            for ref in (ys, gbs, dds):
                ref[tile(m * plane + t * SUB), :] = zero
        return carry

    steps(tokens, 8, clear, 0)
    cells = GROUP * parts

    def some(group, carry):
        first = group * GROUP
        rates = [
            nrates[tile(((first + n) * parts + m) * SUB), :]
            for n in range(GROUP) for m in range(parts)
        ]

        def carried(offset):
            return tuple(
                in_ref[pl.ds(m * SUB * count + offset + first + n, SUB, stride=count), :]
                for n in range(GROUP) for m in range(parts)
            )

        state = carried(0)
        for at in range(cells):
            hs[at * SUB : (at + 1) * SUB, :] = state[at]

        def forward(t, state):
            state = list(state)
            delta, driven, gy, y = (
                [ref[tile(m * plane + t * SUB), :] for m in range(parts)]
                for ref in (dts, dus, gys, ys)
            )
            for n in range(GROUP):
                bb = splat(bs, (first + n) * tokens + t)
                cc = splat(cs, (first + n) * tokens + t)
                pulled = None
                for m in range(parts):
                    at = n * parts + m
                    decay = jnp.exp2(delta[m] * rates[at])
                    now = decay * state[at] + driven[m] * bb
                    state[at] = now
                    hs[tile(((t + 1) * cells + at) * SUB), :] = now
                    y[m] = y[m] + cc * now
                    term = gy[m] * now
                    pulled = term if pulled is None else pulled + term
                pcs[tile((n * tokens + t) * SUB), :] = pulled
            for m in range(parts):
                ys[tile(m * plane + t * SUB), :] = y[m]
            return tuple(state)

        steps(tokens, 32, forward, state)

        def backward(step, carry):
            t = tokens - 1 - step
            back, acc = (list(part) for part in carry)
            delta, driven, gy, gsum, dsum = (
                [ref[tile(m * plane + t * SUB), :] for m in range(parts)]
                for ref in (dts, dus, gys, gbs, dds)
            )
            for n in range(GROUP):
                bb = splat(bs, (first + n) * tokens + t)
                cc = splat(cs, (first + n) * tokens + t)
                pulled = None
                for m in range(parts):
                    at = n * parts + m
                    scaled = delta[m] * rates[at]
                    adj = gy[m] * cc + back[at]
                    gsum[m] = gsum[m] + adj * bb
                    back[at] = jnp.exp2(scaled) * adj
                    both = back[at] * hs[tile((t * cells + at) * SUB), :] * scaled
                    dsum[m] = dsum[m] + both
                    acc[at] = acc[at] + both
                    term = adj * driven[m]
                    pulled = term if pulled is None else pulled + term
                pbs[tile((n * tokens + t) * SUB), :] = pulled
            for m in range(parts):
                gbs[tile(m * plane + t * SUB), :] = gsum[m]
                dds[tile(m * plane + t * SUB), :] = dsum[m]
            return tuple(back), tuple(acc)

        _, acc = steps(tokens, 32, backward, (carried(nstate), (zero,) * cells))
        for n in range(GROUP):
            for m in range(parts):
                base = m * SUB * width + first + n
                par_ref[pl.ds(base, SUB, stride=width), :] = acc[n * parts + m] / -rates[n * parts + m]

        fold(pcs, gc_ref, first * tokens, GROUP * tokens)
        fold(pbs, gb_ref, first * tokens, GROUP * tokens)
        return carry

    lax.fori_loop(0, nstate // GROUP, some, 0)

    for m in range(parts):
        taps_here = [ws[(k * parts + m) * SUB : (k * parts + m + 1) * SUB, :] for k in range(taps)]
        skip = skip_ref[m * SUB : (m + 1) * SUB, :]
        xplane = xs.shape[0] // parts

        def post(t, carry, m=m, skip=skip):
            bias, convb, convw = carry
            here = tile(m * plane + t * SUB)
            gsum, inner = gbs[here, :], us[here, :]
            dd = (gsum * inner + dds[here, :] * (1.0 / LOG2E) / dts[here, :]) * sds[here, :]
            dcv = (gsum * dts[here, :] + gys[here, :] * skip) * sls[here, :]
            dds[here, :] = dd
            gbs[here, :] = dcv
            hs[here, :] = zfs[here, :] * (ys[here, :] + skip * inner)
            convw = tuple(
                convw[k] + dcv * xs[tile(m * xplane + (t + k) * SUB), :] for k in range(taps)
            )
            return bias + dd, convb + dcv, convw

        bias, convb, convw = steps(tokens, 8, post, (zero, zero, (zero,) * taps))
        values = list(convw) + [convb, skipped_ref[m * SUB : (m + 1) * SUB, :], bias]
        for row, value in enumerate(values):
            par_ref[pl.ds(m * SUB * width + nstate + row, SUB, stride=width), :] = value

        def spill(t, carry, m=m, taps_here=taps_here):
            value = None
            for k in range(taps):
                term = taps_here[k] * gbs[tile(m * plane + (t + lead - k) * SUB), :]
                value = term if value is None else value + term
            ys[tile(m * plane + t * SUB), :] = value
            return carry

        whole_steps = (tokens - lead) // 8 * 8
        steps(whole_steps, 8, spill, 0)
        for t in range(whole_steps, tokens - lead):
            spill(t, 0)

        def partial(s):
            value = zero
            for k in range(taps):
                if 0 <= s + lead - k < tokens:
                    value = value + taps_here[k] * gbs[tile(m * plane + (s + lead - k) * SUB), :]
            return value

        for i in range(lead):
            value = partial(tokens - lead + i)
            ys[tile(m * plane + (tokens - lead + i) * SUB), :] = value
            owed_ref[lead + i, m * SUB : (m + 1) * SUB, :] = value
            owed_ref[i, m * SUB : (m + 1) * SUB, :] = partial(i - lead)

    gather_tokens(ys, gx_ref)
    gather_tokens(hs.at[pl.ds(0, parts * plane), :], gz_ref)
    gather_tokens(dds, gd_ref)


def slices(rows, runs):
    blocks, width, lanes = rows.shape
    if blocks % runs == 0:
        return rows.reshape(runs, blocks // runs * width, lanes)
    narrow = blocks * lanes // runs
    return rows.transpose(1, 0, 2).reshape(width, runs, narrow).transpose(1, 0, 2)


def unslices(pieces, blocks, width):
    runs = pieces.shape[0]
    if blocks % runs == 0:
        return pieces.reshape(blocks, width, LANE)
    return pieces.transpose(1, 0, 2).reshape(width, blocks, LANE).transpose(1, 0, 2)


def swap(pieces):
    return lax.all_to_all(pieces, "seq", 0, 0, tiled=True)


def shards(xin, zgate, delta_raw, bmat, cmat, conv_w, conv_b, decay_rate, dskip, dt_bias, grad_out):
    tokens, channels = xin.shape
    nstate, taps = bmat.shape[0], conv_w.shape[0]
    lead = taps - 1
    blocks = channels // LANE
    runs = lax.axis_size("seq")
    me = lax.axis_index("seq")
    mine = max(1, blocks // runs)
    span = channels // runs // mine
    full, edge = tokens * blocks, (tokens + lead) * blocks
    splats, rated = nstate * tokens, nstate * blocks
    vec = lambda rows: pltpu.VMEM((rows, LANE), jnp.float32)
    f32 = lambda *shape: jax.ShapeDtypeStruct(shape, jnp.float32)
    bf16 = lambda *shape: jax.ShapeDtypeStruct(shape, jnp.bfloat16)
    far = lambda *refs: (pltpu.with_memory_space_constraint(ref, pltpu.HBM) for ref in refs)
    limit = lambda mb: pltpu.CompilerParams(vmem_limit_bytes=mb * 1024 * 1024)
    vmem, hbm = (pl.BlockSpec(memory_space=space) for space in (pltpu.VMEM, pltpu.HBM))
    work = nstate * tokens * channels

    def cost(ops, moved):
        return pl.CostEstimate(flops=ops * work, bytes_accessed=moved, transcendentals=work)

    rim = lax.ppermute(
        xin[tokens - lead :].reshape(lead, blocks, LANE), "seq",
        [(i, i + 1) for i in range(runs - 1)],
    )
    cb, dtb, skip = (v.reshape(blocks, LANE) for v in (conv_b, dt_bias, dskip))
    rate_mine = lax.dynamic_slice(decay_rate, (0, me * mine * span), (nstate, mine * span))
    wide = 2 * nstate + 4
    shapes = [full] * 7 + [edge, splats, splats, rated]
    pay, skipped, *factors = pl.pallas_call(
        functools.partial(local_body, tokens, blocks, nstate, taps),
        out_shape=[f32(blocks * wide, LANE), f32(blocks, LANE)] + [vec(r) for r in shapes],
        in_specs=[hbm] * 4 + [vmem] * 7 + [hbm],
        out_specs=[vmem] * 13,
        scratch_shapes=[
            vec(taps * blocks), pltpu.VMEM((4, tokens, channels), jnp.bfloat16),
            pltpu.SemaphoreType.DMA((4,)),
        ],
        compiler_params=limit(LOCAL_MB),
        cost_estimate=cost(9, full * LANE * 36),
        name="local_scan",
    )(
        *far(xin, delta_raw, zgate, grad_out), rim,
        *far(bmat, cmat, conv_w, cb, dtb, decay_rate), rate_mine,
    )
    got = swap(slices(pay.reshape(blocks, wide, LANE), runs))
    carries = pl.pallas_call(
        functools.partial(carry_body, runs, mine, span, nstate, wide),
        out_shape=f32(runs * mine * 2 * nstate, span),
        in_specs=[vmem] * 2,
        out_specs=vmem,
        compiler_params=limit(CARRY_MB),
        name="carry_scan",
    )(got.reshape(runs * mine * wide, span), rate_mine)
    ins = unslices(swap(carries.reshape(runs, mine * 2 * nstate, span)), blocks, 2 * nstate)
    rows = nstate + taps + 3
    rows = rows + (-rows) % SUB
    gx, gz, gd, gb, gc, owed, par = pl.pallas_call(
        functools.partial(grads_body, tokens, blocks, nstate, taps),
        out_shape=(
            bf16(tokens, channels), bf16(tokens, channels), bf16(tokens, channels),
            pltpu.HBM((splats, LANE), jnp.float32), pltpu.HBM((splats, LANE), jnp.float32),
            f32(2 * lead, blocks, LANE), f32(blocks * rows, LANE),
        ),
        in_specs=[vmem] * 15,
        out_specs=tuple([vmem] * 7),
        scratch_shapes=[
            vec(full), vec(full), vec(full), vec((tokens + 1) * GROUP * blocks),
            vec(GROUP * tokens * SUB), vec(GROUP * tokens * SUB), vec(taps * blocks),
        ],
        compiler_params=limit(GRADS_MB),
        cost_estimate=cost(22, nstate * full * LANE),
        name="grads",
    )(ins.reshape(blocks * 2 * nstate, LANE), *far(conv_w, skip), skipped, *factors)
    gb, gc = (jnp.sum(v.reshape(nstate, tokens, LANE), axis=2) for v in (gb, gc))
    returned = lax.ppermute(owed[:lead], "seq", [(i + 1, i) for i in range(runs - 1)])
    last = (owed[lead:] + returned).reshape(lead, channels).astype(jnp.bfloat16)
    gx = lax.dynamic_update_slice(gx, last, (tokens - lead, 0))
    sums = jnp.sum(swap(slices(par.reshape(blocks, rows, LANE), runs)), axis=0)
    every = unslices(swap(jnp.broadcast_to(sums[None], (runs,) + sums.shape)), blocks, rows)
    flat = lambda a, b: every[:, a:b].transpose(1, 0, 2).reshape(b - a, channels)
    line = lambda a: every[:, a].reshape(channels)
    return (
        gx, gz, gd, gb, gc,
        flat(nstate, nstate + taps), line(nstate + taps), flat(0, nstate),
        line(nstate + taps + 1), line(nstate + taps + 2),
    )


def solution(mesh):
    both = P(("dp", "seq"), None)
    across = P(None, ("dp", "seq"))
    return jax.shard_map(
        shards,
        mesh=mesh,
        in_specs=(both, both, both, across, across, P(), P(), P(), P(), P(), both),
        out_specs=(
            both, both, both, across, across,
            P("dp", None), P("dp"), P("dp", None), P("dp"), P("dp"),
        ),
        check_vma=False,
    )
```

time: 162 us -> 139 us (0.86)
  blocking collectives: 35.6 us -> 59.9 us
  Pallas kernels: 75 us -> 55.1 us
  waiting for transfers between devices: 23.5 us -> 7.49 us
  starting transfers between devices: 16.7 us -> 7.2 us
  local copies, waits for them, and re-layouts: 8.01 us -> 5.94 us
    all_to_all x2 -> x3, blocking collectives: 35.6 us -> 59.9 us  [swap(): return lax.all_to_all(pieces, 'seq', 0, 0, tiled=True)]
    all_to_all x2 -> x1, waiting for transfers between devices: 22.6 us -> 7.38 us  [swap(): return lax.all_to_all(pieces, 'seq', 0, 0, tiled=True)]
    pallas_call x1, Pallas kernels: 51.4 us -> 36.9 us  [shards(): pl.pallas_call(functools.partial(grads_body, tokens, blocks, nstate, taps...]
    all_to_all x2 -> x1, starting transfers between devices: 13 us -> 3.55 us  [swap(): return lax.all_to_all(pieces, 'seq', 0, 0, tiled=True)]
    pallas_call x1, Pallas kernels: 21.6 us -> 18.1 us  [shards(): pl.pallas_call(functools.partial(local_body, tokens, blocks, nstate, taps...]
    pallas_call x1, Pallas kernels: 1.96 us -> 0.08 us  [shards(): pl.pallas_call(functools.partial(carry_body, runs, mine, span, nstate, wi...]
  transfers between devices with their start and end apart: 4 -> 3, of which waited for: 3 -> 2; matrix products, arithmetic and copies ran while one was open for 3% -> 3% of each run, Pallas kernels for 0% -> 0%
where the time goes in v2:
time: 139 us; the launch traced here: 138 us
  blocking collectives  59.9 us (43%)
  Pallas kernels  55.1 us (40%)
  waiting for transfers between devices  7.49 us (5%)
  starting transfers between devices  7.2 us (5%)
  local copies, waits for them, and re-layouts  5.94 us (4%)
  other arithmetic  1.92 us (1%)
    all_to_all x3, blocking collectives, swap(): return lax.all_to_all(pieces, 'seq', 0, 0, tiled=True)  59.9 us
    pallas_call x1, Pallas kernels, shards(): pl.pallas_call(functools.partial(grads_body, tokens, blocks, nstate, taps...  36.9 us
    pallas_call x1, Pallas kernels, shards(): pl.pallas_call(functools.partial(local_body, tokens, blocks, nstate, taps...  18.1 us
    all_to_all x1, waiting for transfers between devices, swap(): return lax.all_to_all(pieces, 'seq', 0, 0, tiled=True)  7.38 us
    all_to_all x1, starting transfers between devices, swap(): return lax.all_to_all(pieces, 'seq', 0, 0, tiled=True)  3.55 us
  transfers between devices with their start and end apart: 3, of which 2 were waited for; matrix products, arithmetic and copies ran while one was open for 3% of the time, Pallas kernels for 0%

profile of v2, /device:TPU:0, one launch (start us, length us, event | category | flops | bytes accessed | tf_op | source)
XLA Modules:
  0.0 138.3 jit_solution(2203601883305883978)
XLA Ops:
  0.6 0.9 slice_bitcast_fusion.2
  1.5 2.4 %collective-permute-start = (bf16[3,32,128]{2,1,0:T(8,128)(2,1)S(1)}, bf16[3,32,128]{2,1,0:T(8,128)(2,1)S(1)}, u32[]{:S(2)}, u32[]{:S(2)}) collective-permute-start(bf16[3,32,128]{2,1,0:T(8,128)(2,1)S(1)} %bitcast.43), channel_id=1, source_target_pairs={{0,2},{2,4},{4,6},{6,8},{8,10},{10,12},{12,14},{14,16},{16,18},{18... | collective-permute-start | bytes 73736 | tf_op jit(solution)/shard_map/ppermute | solution.py:434
  3.9 0.7 constant_dynamic-slice_fusion.rate_mine_ref.rate_ref
  4.6 0.1 collective-permute-done.rim_ref
  4.7 18.1 %local_scan.1 = (f32[1152,128]{1,0:T(8,128)S(1)}, f32[32,128]{1,0:T(8,128)S(1)}, f32[4096,128]{1,0:T(8,128)S(1)}, f32[4096,128]{1,0:T(8,128)S(1)}, f32[4096,128]...) custom-call(bf16[128,4096]{1,0:T(8,128)(2,1)} %x_hbm.1, ...), custom_call_target="tpu_custom_call" | custom-call | flops 75497472 | bytes 18874368 | tf_op jit(solution)/shard_map/local_scan/pallas_call | solution.py:442
  22.9 26.4 %all_to_all.20 = f32[16,72,128]{2,1,0:T(8,128)S(1)} all-to-all(f32[16,72,128]{2,1,0:T(8,128)S(1)} %bitcast.37), channel_id=1, replica_groups=mesh['seq'=16,'dp'=2] {'seq'}, dimensions={0} | all-to-all | bytes 1179648 | tf_op jit(solution)/shard_map/all_to_all | solution.py:409
  49.3 0.1 carry_scan.1
  49.4 17.3 %all_to_all.21 = f32[16,64,128]{2,1,0:T(8,128)S(1)} all-to-all(f32[16,64,128]{2,1,0:T(8,128)S(1)} %bitcast.36), channel_id=1, replica_groups=mesh['seq'=16,'dp'=2] {'seq'}, dimensions={0} | all-to-all | bytes 1048576 | tf_op jit(solution)/shard_map/all_to_all | solution.py:409
  66.6 36.9 %grads.1 = (bf16[128,4096]{1,0:T(8,128)(2,1)}, bf16[128,4096]{1,0:T(8,128)(2,1)}, bf16[128,4096]{1,0:T(8,128)(2,1)}, f32[2048,128]{1,0:T(8,128)}, f32[2048,128]{...) custom-call(f32[1024,128]{1,0:T(8,128)S(1)} %bitcast.35, f32[4,4096]{1,0:T(4,128)} %w_ref.3, ...), custom_call_target="tpu_custom_call" | custom-call | flops 184549376 | bytes 8388608 | tf_op jit(solution)/shard_map/grads/pallas_call | solution.py:470
  103.5 0.0 copy-start.1
  103.5 0.0 copy-start
  103.5 16.2 %all_to_all.22 = f32[16,48,128]{2,1,0:T(8,128)S(1)} all-to-all(f32[16,48,128]{2,1,0:T(8,128)S(1)} %bitcast.38), channel_id=1, replica_groups=mesh['seq'=16,'dp'=2] {'seq'}, dimensions={0} | all-to-all | bytes 786432 | tf_op jit(solution)/shard_map/all_to_all | solution.py:409
  119.8 0.8 broadcast_in_dim.2
  120.5 3.6 %all-to-all-start.3 = ((f32[16,48,128]{2,1,0:T(8,128)}), f32[16,48,128]{2,1,0:T(8,128)S(1)}, u32[]{:S(2)}, u32[]{:S(2)}) async-start(f32[16,48,128]{2,1,0:T(8,128)} %broadcast_in_dim.2), calls=%async_computation.3 | async-start | bytes 786432 | tf_op jit(solution)/shard_map/all_to_all | solution.py:409
  124.1 1.3 collective-permute-start.1
  125.4 0.0 copy-done.1
  125.4 0.9 reduce_sum.31
  126.4 0.0 copy-done
  126.4 0.9 reduce_sum.33
  127.3 0.0 collective-permute-done.1
  127.4 1.5 %dynamic_update_slice.3 = bf16[128,4096]{1,0:T(8,128)(2,1)} dynamic-update-slice(bf16[128,4096]{1,0:T(8,128)(2,1)} %get-tuple-element.43, bf16[3,4096]{1,0:T(4,128)(2,1)S(1)} %bitcast.42, s32[]{:T(128)} %constant.16.clone.1, s32[]{:T(128)} %constant.7.clone.1) | dynamic-update-slice | bytes 49156 | tf_op jit(solution)/shard_map/dynamic_update_slice | solution.py:490
  128.9 7.4 %all-to-all-done.3 = f32[16,48,128]{2,1,0:T(8,128)S(1)} async-done(((f32[16,48,128]{2,1,0:T(8,128)}), f32[16,48,128]{2,1,0:T(8,128)S(1)}, u32[]{:S(2)}, u32[]{:S(2)}) %all-to-all-start.3) | async-done | bytes 393248 | tf_op jit(solution)/shard_map/all_to_all | solution.py:409
  136.3 0.6 fusion.1
  136.9 0.6 slice_bitcast_fusion.1
  137.6 0.7 copy_bitcast_fusion
  (5 shorter events, 0.1 us)
Async XLA Ops:
  1.5 3.2 %collective-permute-start = (bf16[3,32,128]{2,1,0:T(8,128)(2,1)S(1)}, bf16[3,32,128]{2,1,0:T(8,128)(2,1)S(1)}, u32[]{:S(2)}, u32[]{:S(2)}) collective-permute-start(bf16[3,32,128]{2,1,0:T(8,128)(2,1)S(1)} %bitcast.43), channel_id=1, source_target_pairs={{0,2},{2,4},{4,6},{6,8},{8,10},{10,12},{12,14},{14,16},{16,18},{18... | collective-permute-start | bytes 73736 | tf_op jit(solution)/shard_map/ppermute | solution.py:434
  103.5 21.9 %copy-start.1 = (f32[2048,128]{1,0:T(8,128)S(1)}, f32[2048,128]{1,0:T(8,128)}, u32[]{:S(2)}) copy-start(f32[2048,128]{1,0:T(8,128)} %get-tuple-element.47) | copy-start | bytes 3145732
  103.5 22.9 %copy-start = (f32[2048,128]{1,0:T(8,128)S(1)}, f32[2048,128]{1,0:T(8,128)}, u32[]{:S(2)}) copy-start(f32[2048,128]{1,0:T(8,128)} %get-tuple-element.48) | copy-start | bytes 3145732
  120.5 15.7 %all-to-all-start.3 = ((f32[16,48,128]{2,1,0:T(8,128)}), f32[16,48,128]{2,1,0:T(8,128)S(1)}, u32[]{:S(2)}, u32[]{:S(2)}) async-start(f32[16,48,128]{2,1,0:T(8,128)} %broadcast_in_dim.2), calls=%async_computation.3 | async-start | bytes 786432 | tf_op jit(solution)/shard_map/all_to_all | solution.py:409
  124.1 3.2 %collective-permute-start.1 = (f32[3,32,128]{2,1,0:T(8,128)S(1)}, f32[3,32,128]{2,1,0:T(8,128)S(1)}, u32[]{:S(2)}, u32[]{:S(2)}) collective-permute-start(f32[3,32,128]{2,1,0:T(8,128)S(1)} %slice.26), channel_id=1, source_target_pairs={{2,0},{4,2},{6,4},{8,6},{10,8},{12,10},{14,12},{16,14},{18,16},{20... | collective-permute-start | bytes 147464 | tf_op jit(solution)/shard_map/ppermute | solution.py:488

commit v3 on v2

--- a/solution.py
+++ b/solution.py
@@ -42,20 +42,19 @@
     lax.fori_loop(0, tokens // 16, some, 0)
 
 
-def gather_tokens(src, dst):
-    tokens, channels = dst.shape
-    blocks = channels // LANE
-    plane = src.shape[0] // (blocks // SUB)
-
+def gather_tokens(pairs):
     def some(group, carry):
         first = pl.multiple_of(group * 16, 16)
-        for blk in range(blocks):
-            start = blk // SUB * plane + blk % SUB + first * SUB
-            piece = src[pl.ds(start, 16, stride=SUB), :]
-            dst[pl.ds(first, 16), blk * LANE : (blk + 1) * LANE] = piece.astype(dst.dtype)
-        return carry
-
-    lax.fori_loop(0, tokens // 16, some, 0)
+        for src, dst in pairs:
+            blocks = dst.shape[1] // LANE
+            plane = src.shape[0] // (blocks // SUB)
+            for blk in range(blocks):
+                start = blk // SUB * plane + blk % SUB + first * SUB
+                piece = src[pl.ds(start, 16, stride=SUB), :]
+                dst[pl.ds(first, 16), blk * LANE : (blk + 1) * LANE] = piece.astype(dst.dtype)
+        return carry
+
+    lax.fori_loop(0, pairs[0][1].shape[0] // 16, some, 0)
 
 
 def place_rim(rim_ref, xs, lead, parts):
@@ -110,59 +109,75 @@
     ]
 
 
-def local_body(
+def prepare_body(
     tokens, blocks, nstate, taps,
-    x_hbm, draw_hbm, z_hbm, go_hbm, rim_ref, b_ref, c_ref, w_ref, cb_ref, dtb_ref, rate_ref,
-    rate_mine_ref,
-    pay_ref, skip_ref, dts, dus, gys, us, zfs, sls, sds, xs, bs, cs, nrates,
-    ws, raw, sems,
+    x_hbm, draw_hbm, z_hbm, go_hbm, b_ref, c_ref, dtb_ref, rate_ref, rate_mine_ref,
+    dts, gys, zfs, sds, xs, bs, cs, nrates,
+    raw, sems,
 ):
-    lead = taps - 1
     parts = blocks // SUB
     plane = tokens * SUB
-    width = pay_ref.shape[0] // blocks
     copies = [
         pltpu.make_async_copy(src, raw.at[i], sems.at[i])
         for i, src in enumerate((draw_hbm, z_hbm, go_hbm, x_hbm))
     ]
     for copy in copies:
         copy.start()
-    spread_rows(w_ref, ws)
     spread_rows(rate_ref, nrates, -LOG2E)
     splat_columns(b_ref, bs, tokens)
     splat_columns(c_ref, cs, tokens)
-    place_rim(rim_ref, xs, lead, parts)
-    for i, (dst, ahead) in enumerate(((dts, 0), (zfs, 0), (gys, 0), (xs, lead))):
+    for i, (dst, ahead) in enumerate(((dts, 0), (zfs, 0), (gys, 0), (xs, taps - 1))):
         copies[i].wait()
         spread_tokens(raw.at[i], dst, ahead)
+
+    for m in range(parts):
+        dtb = dtb_ref[m * SUB : (m + 1) * SUB, :]
+
+        def pre(t, carry, m=m, dtb=dtb):
+            here = tile(m * plane + t * SUB)
+            grow = jnp.exp(dts[here, :] + dtb)
+            zf = zfs[here, :]
+            sig_z = sigmoid(zf)
+            gof = gys[here, :] * sig_z
+            dts[here, :] = jnp.log1p(grow)
+            sds[here, :] = grow / (1.0 + grow)
+            gys[here, :] = gof * zf
+            zfs[here, :] = gof * (1.0 + zf * (1.0 - sig_z))
+            return carry
+
+        steps(tokens, 16, pre, 0)
+
+
+def local_body(
+    tokens, blocks, nstate, taps,
+    rim_ref, w_ref, cb_ref, dts, gys, bs, cs, nrates, xs_in,
+    pay_ref, skip_ref, dus, us, sls, xs,
+    ws,
+):
+    lead = taps - 1
+    parts = blocks // SUB
+    plane = tokens * SUB
+    width = pay_ref.shape[0] // blocks
+    spread_rows(w_ref, ws)
+    place_rim(rim_ref, xs, lead, parts)
     zero = jnp.zeros((SUB, LANE), jnp.float32)
 
     for m in range(parts):
         taps_here = [ws[(k * parts + m) * SUB : (k * parts + m + 1) * SUB, :] for k in range(taps)]
         cb = cb_ref[m * SUB : (m + 1) * SUB, :]
-        dtb = dtb_ref[m * SUB : (m + 1) * SUB, :]
-
-        def pre(t, totals, m=m, taps_here=taps_here, cb=cb, dtb=dtb):
+
+        def pre(t, totals, m=m, taps_here=taps_here, cb=cb):
             here = tile(m * plane + t * SUB)
             conv = conv_at(xs, taps_here, cb, m, t, taps, parts)
             sig_c = sigmoid(conv)
             inner = conv * sig_c
-            grow = jnp.exp(dts[here, :] + dtb)
-            delta = jnp.log1p(grow)
-            zf = zfs[here, :]
-            sig_z = sigmoid(zf)
-            gof = gys[here, :] * sig_z
-            gy = gof * zf
-            gys[here, :] = gy
-            dts[here, :] = delta
+            delta = dts[here, :]
             us[here, :] = inner
             dus[here, :] = delta * inner
-            zfs[here, :] = gof * (1.0 + zf * (1.0 - sig_z))
             sls[here, :] = sig_c * (1.0 + conv * (1.0 - sig_c))
-            sds[here, :] = grow / (1.0 + grow)
-            return totals[0] + delta, totals[1] + gy * inner
-
-        total, skipped = steps(tokens, 8, pre, (zero, zero))
+            return totals[0] + delta, totals[1] + gys[here, :] * inner
+
+        total, skipped = steps(tokens, 16, pre, (zero, zero))
         pay_ref[pl.ds(m * SUB * width + 2 * nstate, SUB, stride=width), :] = total
         skip_ref[m * SUB : (m + 1) * SUB, :] = skipped
 
@@ -188,7 +203,7 @@
 
         count = GROUP * parts
         state, _, pulled = steps(
-            tokens, 32, scan, ((zero,) * count, (one,) * count, (zero,) * count)
+            tokens, 64, scan, ((zero,) * count, (one,) * count, (zero,) * count)
         )
         for n in range(GROUP):
             for m in range(parts):
@@ -229,11 +244,21 @@
     lax.fori_loop(0, count // 64, some, 0)
 
 
+def finish_body(blocks, nstate, taps, every_ref, convw_ref, rate_ref, *line_refs):
+    rows = every_ref.shape[0] // blocks
+    for blk in range(blocks):
+        here = slice(blk * LANE, (blk + 1) * LANE)
+        rate_ref[:, here] = every_ref[blk * rows : blk * rows + nstate, :]
+        convw_ref[:, here] = every_ref[blk * rows + nstate : blk * rows + nstate + taps, :]
+    for i, line_ref in enumerate(line_refs):
+        line_ref[...] = every_ref[pl.ds(nstate + taps + i, blocks, stride=rows), :]
+
+
 def grads_body(
     tokens, blocks, nstate, taps,
     in_ref, w_ref, skip_ref, skipped_ref, dts, dus, gys, us, zfs, sls, sds, xs, bs, cs, nrates,
     gx_ref, gz_ref, gd_ref, gb_ref, gc_ref, owed_ref, par_ref,
-    ys, gbs, dds, hs, pcs, pbs, ws,
+    ys, gbs, dds, hs, pcs, ws,
 ):
     lead = taps - 1
     parts = blocks // SUB
@@ -293,7 +318,8 @@
                 ys[tile(m * plane + t * SUB), :] = y[m]
             return tuple(state)
 
-        steps(tokens, 32, forward, state)
+        steps(tokens, 64, forward, state)
+        fold(pcs, gc_ref, first * tokens, GROUP * tokens)
 
         def backward(step, carry):
             t = tokens - 1 - step
@@ -317,20 +343,18 @@
                     acc[at] = acc[at] + both
                     term = adj * driven[m]
                     pulled = term if pulled is None else pulled + term
-                pbs[tile((n * tokens + t) * SUB), :] = pulled
+                gb_ref[pl.ds((first + n) * tokens + t, 1), :] = jnp.sum(pulled, axis=0, keepdims=True)
             for m in range(parts):
                 gbs[tile(m * plane + t * SUB), :] = gsum[m]
                 dds[tile(m * plane + t * SUB), :] = dsum[m]
             return tuple(back), tuple(acc)
 
-        _, acc = steps(tokens, 32, backward, (carried(nstate), (zero,) * cells))
+        _, acc = steps(tokens, 64, backward, (carried(nstate), (zero,) * cells))
         for n in range(GROUP):
             for m in range(parts):
                 base = m * SUB * width + first + n
                 par_ref[pl.ds(base, SUB, stride=width), :] = acc[n * parts + m] / -rates[n * parts + m]
 
-        fold(pcs, gc_ref, first * tokens, GROUP * tokens)
-        fold(pbs, gb_ref, first * tokens, GROUP * tokens)
         return carry
 
     lax.fori_loop(0, nstate // GROUP, some, 0)
@@ -354,7 +378,7 @@
             )
             return bias + dd, convb + dcv, convw
 
-        bias, convb, convw = steps(tokens, 8, post, (zero, zero, (zero,) * taps))
+        bias, convb, convw = steps(tokens, 16, post, (zero, zero, (zero,) * taps))
         values = list(convw) + [convb, skipped_ref[m * SUB : (m + 1) * SUB, :], bias]
         for row, value in enumerate(values):
             par_ref[pl.ds(m * SUB * width + nstate + row, SUB, stride=width), :] = value
@@ -385,9 +409,7 @@
             owed_ref[lead + i, m * SUB : (m + 1) * SUB, :] = value
             owed_ref[i, m * SUB : (m + 1) * SUB, :] = partial(i - lead)
 
-    gather_tokens(ys, gx_ref)
-    gather_tokens(hs.at[pl.ds(0, parts * plane), :], gz_ref)
-    gather_tokens(dds, gd_ref)
+    gather_tokens(((ys, gx_ref), (hs.at[pl.ds(0, parts * plane), :], gz_ref), (dds, gd_ref)))
 
 
 def slices(rows, runs):
@@ -438,23 +460,33 @@
     cb, dtb, skip = (v.reshape(blocks, LANE) for v in (conv_b, dt_bias, dskip))
     rate_mine = lax.dynamic_slice(decay_rate, (0, me * mine * span), (nstate, mine * span))
     wide = 2 * nstate + 4
-    shapes = [full] * 7 + [edge, splats, splats, rated]
-    pay, skipped, *factors = pl.pallas_call(
+    dts, gys, zfs, sds, xs, bs, cs, nrates = pl.pallas_call(
+        functools.partial(prepare_body, tokens, blocks, nstate, taps),
+        out_shape=[vec(r) for r in [full] * 4 + [edge, splats, splats, rated]],
+        in_specs=[hbm] * 4 + [vmem] * 4 + [hbm],
+        out_specs=[vmem] * 8,
+        scratch_shapes=[
+            pltpu.VMEM((4, tokens, channels), jnp.bfloat16), pltpu.SemaphoreType.DMA((4,)),
+        ],
+        compiler_params=limit(LOCAL_MB),
+        cost_estimate=cost(3, full * LANE * 8),
+        name="prepare",
+    )(
+        *far(xin, delta_raw, zgate, grad_out, bmat, cmat, dtb, decay_rate), rate_mine
+    )
+    pay, skipped, dus, us, sls, xs = pl.pallas_call(
         functools.partial(local_body, tokens, blocks, nstate, taps),
-        out_shape=[f32(blocks * wide, LANE), f32(blocks, LANE)] + [vec(r) for r in shapes],
-        in_specs=[hbm] * 4 + [vmem] * 7 + [hbm],
-        out_specs=[vmem] * 13,
-        scratch_shapes=[
-            vec(taps * blocks), pltpu.VMEM((4, tokens, channels), jnp.bfloat16),
-            pltpu.SemaphoreType.DMA((4,)),
-        ],
+        out_shape=[f32(blocks * wide, LANE), f32(blocks, LANE)]
+        + [vec(r) for r in [full] * 3 + [edge]],
+        in_specs=[vmem] * 9,
+        out_specs=[vmem] * 6,
+        scratch_shapes=[vec(taps * blocks)],
+        input_output_aliases={8: 5},
         compiler_params=limit(LOCAL_MB),
         cost_estimate=cost(9, full * LANE * 36),
         name="local_scan",
-    )(
-        *far(xin, delta_raw, zgate, grad_out), rim,
-        *far(bmat, cmat, conv_w, cb, dtb, decay_rate), rate_mine,
-    )
+    )(rim, *far(conv_w, cb), dts, gys, bs, cs, nrates, xs)
+    factors = (dts, dus, gys, us, zfs, sls, sds, xs, bs, cs, nrates)
     got = swap(slices(pay.reshape(blocks, wide, LANE), runs))
     carries = pl.pallas_call(
         functools.partial(carry_body, runs, mine, span, nstate, wide),
@@ -478,7 +510,8 @@
         out_specs=tuple([vmem] * 7),
         scratch_shapes=[
             vec(full), vec(full), vec(full), vec((tokens + 1) * GROUP * blocks),
-            vec(GROUP * tokens * SUB), vec(GROUP * tokens * SUB), vec(taps * blocks),
+            vec(GROUP * tokens * SUB),
+            vec(taps * blocks),
         ],
         compiler_params=limit(GRADS_MB),
         cost_estimate=cost(22, nstate * full * LANE),
@@ -490,13 +523,16 @@
     gx = lax.dynamic_update_slice(gx, last, (tokens - lead, 0))
     sums = jnp.sum(swap(slices(par.reshape(blocks, rows, LANE), runs)), axis=0)
     every = unslices(swap(jnp.broadcast_to(sums[None], (runs,) + sums.shape)), blocks, rows)
-    flat = lambda a, b: every[:, a:b].transpose(1, 0, 2).reshape(b - a, channels)
-    line = lambda a: every[:, a].reshape(channels)
-    return (
-        gx, gz, gd, gb, gc,
-        flat(nstate, nstate + taps), line(nstate + taps), flat(0, nstate),
-        line(nstate + taps + 1), line(nstate + taps + 2),
-    )
+    convw, rate, *lines = pl.pallas_call(
+        functools.partial(finish_body, blocks, nstate, taps),
+        out_shape=[f32(taps, channels), f32(nstate, channels)] + [f32(blocks, LANE)] * 3,
+        in_specs=[vmem],
+        out_specs=[vmem] * 5,
+        compiler_params=limit(CARRY_MB),
+        name="finish",
+    )(every.reshape(blocks * rows, LANE))
+    convb, skips, bias = (v.reshape(channels) for v in lines)
+    return gx, gz, gd, gb, gc, convw, convb, rate, skips, bias
 
 
 def solution(mesh):

time: 139 us -> 135 us (0.971)
  blocking collectives: 59.9 us -> 57.8 us
  local copies, waits for them, and re-layouts: 5.94 us -> 3.93 us
    pallas_call x0 -> x2, Pallas kernels: none -> 6.73 us  [the longest x1 5.97 us: shards(): pl.pallas_call(functools.partial(prepare_body, tokens, blocks, nstate, ta...]
    pallas_call x1, Pallas kernels: 18.1 us -> 12.8 us  [shards(): pl.pallas_call(functools.partial(local_body, tokens, blocks, nstate, taps...]
    all_to_all x3, blocking collectives: 59.9 us -> 57.8 us  [swap(): return lax.all_to_all(pieces, 'seq', 0, 0, tiled=True)]
  transfers between devices with their start and end apart: 3 -> 3, of which waited for: 2 -> 1; matrix products, arithmetic and copies ran while one was open for 3% -> 3% of each run, Pallas kernels for 0% -> 4%
where the time goes in v3:
time: 135 us
  blocking collectives  57.8 us (43%)
  Pallas kernels  55.6 us (41%)
  waiting for transfers between devices  7.39 us (5%)
  starting transfers between devices  7.2 us (5%)
  local copies, waits for them, and re-layouts  3.93 us (3%)
  other arithmetic  1.92 us (1%)
    all_to_all x3, blocking collectives, swap(): return lax.all_to_all(pieces, 'seq', 0, 0, tiled=True)  57.8 us
    pallas_call x1, Pallas kernels, shards(): pl.pallas_call(functools.partial(grads_body, tokens, blocks, nstate, taps...  35.9 us
    pallas_call x1, Pallas kernels, shards(): pl.pallas_call(functools.partial(local_body, tokens, blocks, nstate, taps...  12.8 us
    all_to_all x1, waiting for transfers between devices, swap(): return lax.all_to_all(pieces, 'seq', 0, 0, tiled=True)  7.38 us
    pallas_call x1, Pallas kernels, shards(): pl.pallas_call(functools.partial(prepare_body, tokens, blocks, nstate, ta...  5.97 us
    all_to_all x1, starting transfers between devices, swap(): return lax.all_to_all(pieces, 'seq', 0, 0, tiled=True)  3.55 us
  transfers between devices with their start and end apart: 3, of which 1 were waited for; matrix products, arithmetic and copies ran while one was open for 3% of the time, Pallas kernels for 4%

profile of v3, /device:TPU:0, one launch (start us, length us, event | category | flops | bytes accessed | tf_op | source)
XLA Modules:
  0.0 134.6 jit_solution(13058441417233411293)
XLA Ops:
  0.6 0.9 slice_bitcast_fusion
  1.5 2.4 %collective-permute-start = (bf16[3,32,128]{2,1,0:T(8,128)(2,1)S(1)}, bf16[3,32,128]{2,1,0:T(8,128)(2,1)S(1)}, u32[]{:S(2)}, u32[]{:S(2)}) collective-permute-start(bf16[3,32,128]{2,1,0:T(8,128)(2,1)S(1)} %bitcast.31), channel_id=1, source_target_pairs={{0,2},{2,4},{4,6},{6,8},{8,10},{10,12},{12,14},{14,16},{16,18},{18... | collective-permute-start | bytes 73736 | tf_op jit(solution)/shard_map/ppermute | solution.py:456
  3.9 0.7 constant_dynamic-slice_fusion.rate_mine_ref.rate_ref
  4.6 6.0 %prepare.1 = (f32[4096,128]{1,0:T(8,128)S(1)}, f32[4096,128]{1,0:T(8,128)S(1)}, f32[4096,128]{1,0:T(8,128)S(1)}, f32[4096,128]{1,0:T(8,128)S(1)}, f32[4192,128]{...) custom-call(bf16[128,4096]{1,0:T(8,128)(2,1)} %x_hbm.1, ...), custom_call_target="tpu_custom_call" | custom-call | flops 25165824 | bytes 4194304 | tf_op jit(solution)/shard_map/prepare/pallas_call | solution.py:463
  10.6 0.0 collective-permute-done.rim_ref
  10.6 12.8 %local_scan.1 = (f32[1152,128]{1,0:T(8,128)S(1)}, f32[32,128]{1,0:T(8,128)S(1)}, f32[4096,128]{1,0:T(8,128)S(1)}, f32[4096,128]{1,0:T(8,128)S(1)}, f32[4096,128]{1,0:T(8,128)S(1)}, /*index=5*/f32[4192,128]{1,0:T(8,128)S(1)}) custom-call(bf16[3,32,128]{2,1,0:T(8,128)(2,1)S(1)} %collective-permute-done.rim_ref, ...), custom_call_target="tpu_custom_call", output_to_operand_aliasing={{5}: (8, {})} | custom-call | flops 75497472 | bytes 18874368 | tf_op jit(solution)/shard_map/local_scan/pallas_call | solution.py:477
  23.5 24.3 %all_to_all.20 = f32[16,72,128]{2,1,0:T(8,128)S(1)} all-to-all(f32[16,72,128]{2,1,0:T(8,128)S(1)} %bitcast.28), channel_id=1, replica_groups=mesh['seq'=16,'dp'=2] {'seq'}, dimensions={0} | all-to-all | bytes 1179648 | tf_op jit(solution)/shard_map/all_to_all | solution.py:431
  47.8 0.1 carry_scan.1
  47.8 17.3 %all_to_all.21 = f32[16,64,128]{2,1,0:T(8,128)S(1)} all-to-all(f32[16,64,128]{2,1,0:T(8,128)S(1)} %bitcast.26), channel_id=1, replica_groups=mesh['seq'=16,'dp'=2] {'seq'}, dimensions={0} | all-to-all | bytes 1048576 | tf_op jit(solution)/shard_map/all_to_all | solution.py:431
  65.1 35.9 %grads.1 = (bf16[128,4096]{1,0:T(8,128)(2,1)}, bf16[128,4096]{1,0:T(8,128)(2,1)}, bf16[128,4096]{1,0:T(8,128)(2,1)}, f32[2048,128]{1,0:T(8,128)}, f32[2048,128]{...) custom-call(f32[1024,128]{1,0:T(8,128)S(1)} %bitcast.25, f32[4,4096]{1,0:T(4,128)} %w_ref.3, ...), custom_call_target="tpu_custom_call" | custom-call | flops 184549376 | bytes 8388608 | tf_op jit(solution)/shard_map/grads/pallas_call | solution.py:502
  101.0 0.0 copy-start.1
  101.0 0.0 copy-start
  101.0 16.2 %all_to_all.22 = f32[16,48,128]{2,1,0:T(8,128)S(1)} all-to-all(f32[16,48,128]{2,1,0:T(8,128)S(1)} %bitcast.29), channel_id=1, replica_groups=mesh['seq'=16,'dp'=2] {'seq'}, dimensions={0} | all-to-all | bytes 786432 | tf_op jit(solution)/shard_map/all_to_all | solution.py:431
  117.3 0.8 broadcast_in_dim.2
  118.1 3.6 %all-to-all-start.3 = ((f32[16,48,128]{2,1,0:T(8,128)}), f32[16,48,128]{2,1,0:T(8,128)S(1)}, u32[]{:S(2)}, u32[]{:S(2)}) async-start(f32[16,48,128]{2,1,0:T(8,128)} %broadcast_in_dim.2), calls=%async_computation.3 | async-start | bytes 786432 | tf_op jit(solution)/shard_map/all_to_all | solution.py:431
  121.6 1.3 collective-permute-start.1
  122.9 0.0 copy-done.1
  123.0 0.9 reduce_sum.31
  123.9 0.0 copy-done
  123.9 0.9 reduce_sum.33
  124.8 0.0 collective-permute-done.1
  124.9 1.5 %dynamic_update_slice.3 = bf16[128,4096]{1,0:T(8,128)(2,1)} dynamic-update-slice(bf16[128,4096]{1,0:T(8,128)(2,1)} %get-tuple-element.50, bf16[3,4096]{1,0:T(4,128)(2,1)S(1)} %bitcast.30, s32[]{:T(128)} %constant.16.clone.1, s32[]{:T(128)} %constant.7.clone.1) | dynamic-update-slice | bytes 49156 | tf_op jit(solution)/shard_map/dynamic_update_slice | solution.py:523
  126.4 7.4 %all-to-all-done.3 = f32[16,48,128]{2,1,0:T(8,128)S(1)} async-done(((f32[16,48,128]{2,1,0:T(8,128)}), f32[16,48,128]{2,1,0:T(8,128)S(1)}, u32[]{:S(2)}, u32[]{:S(2)}) %all-to-all-start.3) | async-done | bytes 393248 | tf_op jit(solution)/shard_map/all_to_all | solution.py:431
  133.8 0.8 finish.1
  (5 shorter events, 0.1 us)
Async XLA Ops:
  1.5 9.1 %collective-permute-start = (bf16[3,32,128]{2,1,0:T(8,128)(2,1)S(1)}, bf16[3,32,128]{2,1,0:T(8,128)(2,1)S(1)}, u32[]{:S(2)}, u32[]{:S(2)}) collective-permute-start(bf16[3,32,128]{2,1,0:T(8,128)(2,1)S(1)} %bitcast.31), channel_id=1, source_target_pairs={{0,2},{2,4},{4,6},{6,8},{8,10},{10,12},{12,14},{14,16},{16,18},{18... | collective-permute-start | bytes 73736 | tf_op jit(solution)/shard_map/ppermute | solution.py:456
  101.0 21.9 %copy-start.1 = (f32[2048,128]{1,0:T(8,128)S(1)}, f32[2048,128]{1,0:T(8,128)}, u32[]{:S(2)}) copy-start(f32[2048,128]{1,0:T(8,128)} %get-tuple-element.54) | copy-start | bytes 3145732
  101.0 22.9 %copy-start = (f32[2048,128]{1,0:T(8,128)S(1)}, f32[2048,128]{1,0:T(8,128)}, u32[]{:S(2)}) copy-start(f32[2048,128]{1,0:T(8,128)} %get-tuple-element.55) | copy-start | bytes 3145732
  118.1 15.7 %all-to-all-start.3 = ((f32[16,48,128]{2,1,0:T(8,128)}), f32[16,48,128]{2,1,0:T(8,128)S(1)}, u32[]{:S(2)}, u32[]{:S(2)}) async-start(f32[16,48,128]{2,1,0:T(8,128)} %broadcast_in_dim.2), calls=%async_computation.3 | async-start | bytes 786432 | tf_op jit(solution)/shard_map/all_to_all | solution.py:431
  121.6 3.2 %collective-permute-start.1 = (f32[3,32,128]{2,1,0:T(8,128)S(1)}, f32[3,32,128]{2,1,0:T(8,128)S(1)}, u32[]{:S(2)}, u32[]{:S(2)}) collective-permute-start(f32[3,32,128]{2,1,0:T(8,128)S(1)} %slice.11), channel_id=1, source_target_pairs={{2,0},{4,2},{6,4},{8,6},{10,8},{12,10},{14,12},{16,14},{18,16},{20... | collective-permute-start | bytes 147464 | tf_op jit(solution)/shard_map/ppermute | solution.py:521

commit v4 on v3

--- a/solution.py
+++ b/solution.py
@@ -11,7 +11,7 @@
 LANE = 128
 SUB = 8
 LOG2E = math.log2(math.e)
-LOCAL_MB, CARRY_MB, GRADS_MB = 20, 2, 30
+LOCAL_MB, CARRY_MB, GRADS_MB = 20, 2, 36
 
 
 def tile(start):
@@ -256,9 +256,9 @@
 
 def grads_body(
     tokens, blocks, nstate, taps,
-    in_ref, w_ref, skip_ref, skipped_ref, dts, dus, gys, us, zfs, sls, sds, xs, bs, cs, nrates,
-    gx_ref, gz_ref, gd_ref, gb_ref, gc_ref, owed_ref, par_ref,
-    ys, gbs, dds, hs, pcs, ws,
+    in_ref, skip_ref, skipped_ref, dts, dus, gys, us, zfs, sls, sds, xs, bs, cs, nrates,
+    dcv_hbm, gz_hbm, dd_hbm, gb_hbm, gc_ref, par_ref,
+    ys, gbs, dds, hs, pcs, pbs, sems, sum_sems,
 ):
     lead = taps - 1
     parts = blocks // SUB
@@ -266,7 +266,6 @@
     count = in_ref.shape[0] // blocks
     width = par_ref.shape[0] // blocks
     zero = jnp.zeros((SUB, LANE), jnp.float32)
-    spread_rows(w_ref, ws)
 
     def clear(t, carry):
         for m in range(parts):
@@ -276,6 +275,11 @@
 
     steps(tokens, 8, clear, 0)
     cells = GROUP * parts
+    share = GROUP * tokens * SUB
+
+    def leave(group):
+        here = pl.ds(pl.multiple_of(group * share, SUB), share)
+        return pltpu.make_async_copy(pbs.at[here, :], gb_hbm.at[here, :], sum_sems.at[group])
 
     def some(group, carry):
         first = group * GROUP
@@ -343,7 +347,7 @@
                     acc[at] = acc[at] + both
                     term = adj * driven[m]
                     pulled = term if pulled is None else pulled + term
-                gb_ref[pl.ds((first + n) * tokens + t, 1), :] = jnp.sum(pulled, axis=0, keepdims=True)
+                pbs[tile(((first + n) * tokens + t) * SUB), :] = pulled
             for m in range(parts):
                 gbs[tile(m * plane + t * SUB), :] = gsum[m]
                 dds[tile(m * plane + t * SUB), :] = dsum[m]
@@ -355,12 +359,13 @@
                 base = m * SUB * width + first + n
                 par_ref[pl.ds(base, SUB, stride=width), :] = acc[n * parts + m] / -rates[n * parts + m]
 
+        leave(group).start()
         return carry
 
     lax.fori_loop(0, nstate // GROUP, some, 0)
 
+    copies = []
     for m in range(parts):
-        taps_here = [ws[(k * parts + m) * SUB : (k * parts + m + 1) * SUB, :] for k in range(taps)]
         skip = skip_ref[m * SUB : (m + 1) * SUB, :]
         xplane = xs.shape[0] // parts
 
@@ -383,6 +388,38 @@
         for row, value in enumerate(values):
             par_ref[pl.ds(m * SUB * width + nstate + row, SUB, stride=width), :] = value
 
+        here = pl.ds(m * plane, plane)
+        for i, (src, dst) in enumerate(((gbs, dcv_hbm), (hs, gz_hbm), (dds, dd_hbm))):
+            copies.append(pltpu.make_async_copy(src.at[here, :], dst.at[here, :], sems.at[m, i]))
+            copies[-1].start()
+
+    for copy in copies:
+        copy.wait()
+    for group in range(nstate // GROUP):
+        leave(group).wait()
+
+
+def outs_body(
+    tokens, blocks, taps,
+    w_ref, dcv_hbm, gz_hbm, dd_hbm,
+    gx_ref, gz_ref, gd_ref, owed_ref,
+    gbs, gzs, dds, ys, ws, sems,
+):
+    lead = taps - 1
+    parts = blocks // SUB
+    plane = tokens * SUB
+    zero = jnp.zeros((SUB, LANE), jnp.float32)
+    copies = [
+        pltpu.make_async_copy(src, dst, sems.at[i])
+        for i, (src, dst) in enumerate(((dcv_hbm, gbs), (gz_hbm, gzs), (dd_hbm, dds)))
+    ]
+    for copy in copies:
+        copy.start()
+    spread_rows(w_ref, ws)
+    copies[0].wait()
+    for m in range(parts):
+        taps_here = [ws[(k * parts + m) * SUB : (k * parts + m + 1) * SUB, :] for k in range(taps)]
+
         def spill(t, carry, m=m, taps_here=taps_here):
             value = None
             for k in range(taps):
@@ -409,7 +446,9 @@
             owed_ref[lead + i, m * SUB : (m + 1) * SUB, :] = value
             owed_ref[i, m * SUB : (m + 1) * SUB, :] = partial(i - lead)
 
-    gather_tokens(((ys, gx_ref), (hs.at[pl.ds(0, parts * plane), :], gz_ref), (dds, gd_ref)))
+    copies[1].wait()
+    copies[2].wait()
+    gather_tokens(((ys, gx_ref), (gzs, gz_ref), (dds, gd_ref)))
 
 
 def slices(rows, runs):
@@ -499,29 +538,44 @@
     ins = unslices(swap(carries.reshape(runs, mine * 2 * nstate, span)), blocks, 2 * nstate)
     rows = nstate + taps + 3
     rows = rows + (-rows) % SUB
-    gx, gz, gd, gb, gc, owed, par = pl.pallas_call(
+    away = lambda rows: pltpu.HBM((rows, LANE), jnp.float32)
+    dcv, gz, dd, gb, gc, par = pl.pallas_call(
         functools.partial(grads_body, tokens, blocks, nstate, taps),
-        out_shape=(
-            bf16(tokens, channels), bf16(tokens, channels), bf16(tokens, channels),
-            pltpu.HBM((splats, LANE), jnp.float32), pltpu.HBM((splats, LANE), jnp.float32),
-            f32(2 * lead, blocks, LANE), f32(blocks * rows, LANE),
-        ),
-        in_specs=[vmem] * 15,
-        out_specs=tuple([vmem] * 7),
+        out_shape=(*[away(full)] * 3, away(splats * SUB), away(splats), f32(blocks * rows, LANE)),
+        in_specs=[vmem] * 14,
+        out_specs=(*[hbm] * 4, vmem, vmem),
         scratch_shapes=[
             vec(full), vec(full), vec(full), vec((tokens + 1) * GROUP * blocks),
-            vec(GROUP * tokens * SUB),
-            vec(taps * blocks),
+            vec(GROUP * tokens * SUB), vec(splats * SUB), pltpu.SemaphoreType.DMA((blocks // SUB, 3)),
+            pltpu.SemaphoreType.DMA((nstate // GROUP,)),
         ],
         compiler_params=limit(GRADS_MB),
         cost_estimate=cost(22, nstate * full * LANE),
         name="grads",
-    )(ins.reshape(blocks * 2 * nstate, LANE), *far(conv_w, skip), skipped, *factors)
-    gb, gc = (jnp.sum(v.reshape(nstate, tokens, LANE), axis=2) for v in (gb, gc))
+    )(ins.reshape(blocks * 2 * nstate, LANE), *far(skip), skipped, *factors)
+    summed = swap(slices(par.reshape(blocks, rows, LANE), runs))
+    gx, gz, gd, owed = pl.pallas_call(
+        functools.partial(outs_body, tokens, blocks, taps),
+        out_shape=(*[pltpu.HBM((tokens, channels), jnp.bfloat16)] * 3, f32(2 * lead, blocks, LANE)),
+        in_specs=[vmem] + [hbm] * 3,
+        out_specs=tuple([vmem] * 4),
+        scratch_shapes=[
+            vec(full), vec(full), vec(full), vec(full), vec(taps * blocks),
+            pltpu.SemaphoreType.DMA((3,)),
+        ],
+        compiler_params=limit(GRADS_MB),
+        cost_estimate=pl.CostEstimate(
+            flops=8 * full * LANE, bytes_accessed=5 * full * LANE * 4, transcendentals=0
+        ),
+        name="outs",
+    )(*far(conv_w, dcv, gz, dd))
+    sums = jnp.sum(summed, axis=0)
+    gc = jnp.sum(gc.reshape(nstate, tokens, LANE), axis=2)
+    sums, owed, gc = lax.optimization_barrier((sums, owed, gc))
+    gb = jnp.sum(gb.reshape(nstate, tokens, SUB, LANE), axis=(2, 3))
     returned = lax.ppermute(owed[:lead], "seq", [(i + 1, i) for i in range(runs - 1)])
     last = (owed[lead:] + returned).reshape(lead, channels).astype(jnp.bfloat16)
     gx = lax.dynamic_update_slice(gx, last, (tokens - lead, 0))
-    sums = jnp.sum(swap(slices(par.reshape(blocks, rows, LANE), runs)), axis=0)
     every = unslices(swap(jnp.broadcast_to(sums[None], (runs,) + sums.shape)), blocks, rows)
     convw, rate, *lines = pl.pallas_call(
         functools.partial(finish_body, blocks, nstate, taps),

time: 135 us -> 133 us (0.985)
  blocking collectives: 57.8 us -> 41.6 us
  other arithmetic: 1.92 us -> 7.79 us
  Pallas kernels: 55.6 us -> 59.7 us
  starting transfers between devices: 7.2 us -> 11.3 us
    all_to_all x3 -> x2, blocking collectives: 57.8 us -> 41.6 us  [swap(): return lax.all_to_all(pieces, 'seq', 0, 0, tiled=True)]
    pallas_call x0 -> x1, Pallas kernels: none -> 6.62 us  [shards(): pl.pallas_call(functools.partial(outs_body, tokens, blocks, taps), out_sh...]
    reduce_sum x3 -> x4, other arithmetic: 1.91 us -> 7.78 us  [the longest x2 5.58 us: shards(): gb = jnp.sum(gb.reshape(nstate, tokens, SUB, LANE), axis=(2, 3))]
    all_to_all x1 -> x2, starting transfers between devices: 3.55 us -> 7.66 us  [swap(): return lax.all_to_all(pieces, 'seq', 0, 0, tiled=True)]
    pallas_call x1, Pallas kernels: 35.9 us -> 33.4 us  [shards(): pl.pallas_call(functools.partial(grads_body, tokens, blocks, nstate, taps...]
    all_to_all x1 -> x2, waiting for transfers between devices: 7.38 us -> 6.52 us  [swap(): return lax.all_to_all(pieces, 'seq', 0, 0, tiled=True)]
  transfers between devices with their start and end apart: 3 -> 4, of which waited for: 1 -> 2; matrix products, arithmetic and copies ran while one was open for 3% -> 8% of each run, Pallas kernels for 4% -> 10%
where the time goes in v4:
time: 133 us; the launch traced here: 132 us
  Pallas kernels  59.7 us (45%)
  blocking collectives  41.6 us (31%)
  starting transfers between devices  11.3 us (8%)
  other arithmetic  7.79 us (6%)
  waiting for transfers between devices  6.52 us (5%)
  local copies, waits for them, and re-layouts  4.53 us (3%)
    all_to_all x2, blocking collectives, swap(): return lax.all_to_all(pieces, 'seq', 0, 0, tiled=True)  41.6 us
    pallas_call x1, Pallas kernels, shards(): pl.pallas_call(functools.partial(grads_body, tokens, blocks, nstate, taps...  33.4 us
    pallas_call x1, Pallas kernels, shards(): pl.pallas_call(functools.partial(local_body, tokens, blocks, nstate, taps...  12.8 us
    all_to_all x2, starting transfers between devices, swap(): return lax.all_to_all(pieces, 'seq', 0, 0, tiled=True)  7.66 us
    pallas_call x1, Pallas kernels, shards(): pl.pallas_call(functools.partial(outs_body, tokens, blocks, taps), out_sh...  6.62 us
    all_to_all x2, waiting for transfers between devices, swap(): return lax.all_to_all(pieces, 'seq', 0, 0, tiled=True)  6.52 us
    pallas_call x1, Pallas kernels, shards(): pl.pallas_call(functools.partial(prepare_body, tokens, blocks, nstate, ta...  5.97 us
    reduce_sum x2, other arithmetic, shards(): gb = jnp.sum(gb.reshape(nstate, tokens, SUB, LANE), axis=(2, 3))  5.58 us
  transfers between devices with their start and end apart: 4, of which 2 were waited for; matrix products, arithmetic and copies ran while one was open for 8% of the time, Pallas kernels for 10%

profile of v4, /device:TPU:0, one launch (start us, length us, event | category | flops | bytes accessed | tf_op | source)
XLA Modules:
  0.0 132.2 jit_solution(1892350406959200588)
XLA Ops:
  0.6 0.9 slice_bitcast_fusion
  1.5 2.4 %collective-permute-start = (bf16[3,32,128]{2,1,0:T(8,128)(2,1)S(1)}, bf16[3,32,128]{2,1,0:T(8,128)(2,1)S(1)}, u32[]{:S(2)}, u32[]{:S(2)}) collective-permute-start(bf16[3,32,128]{2,1,0:T(8,128)(2,1)S(1)} %bitcast.29), channel_id=1, source_target_pairs={{0,2},{2,4},{4,6},{6,8},{8,10},{10,12},{12,14},{14,16},{16,18},{18... | collective-permute-start | bytes 73736 | tf_op jit(solution)/shard_map/ppermute | solution.py:495
  3.9 0.7 constant_dynamic-slice_fusion.rate_mine_ref.rate_ref
  4.6 6.0 %prepare.1 = (f32[4096,128]{1,0:T(8,128)S(1)}, f32[4096,128]{1,0:T(8,128)S(1)}, f32[4096,128]{1,0:T(8,128)S(1)}, f32[4096,128]{1,0:T(8,128)S(1)}, f32[4192,128]{...) custom-call(bf16[128,4096]{1,0:T(8,128)(2,1)} %x_hbm.1, ...), custom_call_target="tpu_custom_call" | custom-call | flops 25165824 | bytes 4194304 | tf_op jit(solution)/shard_map/prepare/pallas_call | solution.py:502
  10.6 0.0 collective-permute-done.rim_ref
  10.6 12.8 %local_scan.1 = (f32[1152,128]{1,0:T(8,128)S(1)}, f32[32,128]{1,0:T(8,128)S(1)}, f32[4096,128]{1,0:T(8,128)S(1)}, f32[4096,128]{1,0:T(8,128)S(1)}, f32[4096,128]{1,0:T(8,128)S(1)}, /*index=5*/f32[4192,128]{1,0:T(8,128)S(1)}) custom-call(bf16[3,32,128]{2,1,0:T(8,128)(2,1)S(1)} %collective-permute-done.rim_ref, ...), custom_call_target="tpu_custom_call", output_to_operand_aliasing={{5}: (8, {})} | custom-call | flops 75497472 | bytes 18874368 | tf_op jit(solution)/shard_map/local_scan/pallas_call | solution.py:516
  23.5 0.0 copy-start
  23.5 24.3 %all_to_all.20 = f32[16,72,128]{2,1,0:T(8,128)S(1)} all-to-all(f32[16,72,128]{2,1,0:T(8,128)S(1)} %bitcast.27), channel_id=1, replica_groups=mesh['seq'=16,'dp'=2] {'seq'}, dimensions={0} | all-to-all | bytes 1179648 | tf_op jit(solution)/shard_map/all_to_all | solution.py:470
  47.8 0.1 carry_scan.1
  47.9 17.3 %all_to_all.21 = f32[16,64,128]{2,1,0:T(8,128)S(1)} all-to-all(f32[16,64,128]{2,1,0:T(8,128)S(1)} %bitcast.25), channel_id=1, replica_groups=mesh['seq'=16,'dp'=2] {'seq'}, dimensions={0} | all-to-all | bytes 1048576 | tf_op jit(solution)/shard_map/all_to_all | solution.py:470
  65.1 0.0 copy-done
  65.1 33.4 %grads.1 = (f32[4096,128]{1,0:T(8,128)}, f32[4096,128]{1,0:T(8,128)}, f32[4096,128]{1,0:T(8,128)}, f32[16384,128]{1,0:T(8,128)}, f32[2048,128]{1,0:T(8,128)}, /*index=5*/f32[768,128]{1,0:T(8,128)}) custom-call(f32[1024,128]{1,0:T(8,128)S(1)} %bitcast.24, f32[32,128]{1,0:T(8,128)} %bitcast.30, f32[32,128]{1,0:T(8,128)S(1)} %get-tuple-element.49.skipped_ref, ...), custom_call_target="tpu_custom_call" | custom-call | flops 184549376 | bytes 8388608 | tf_op jit(solution)/shard_map/grads/pallas_call | solution.py:542
  98.5 4.1 %all-to-all-start.2 = ((f32[16,48,128]{2,1,0:T(8,128)}), f32[16,48,128]{2,1,0:T(8,128)S(1)}, u32[]{:S(2)}, u32[]{:S(2)}) async-start(f32[16,48,128]{2,1,0:T(8,128)} %bitcast.7), calls=%async_computation.2 | async-start | bytes 786432 | tf_op jit(solution)/shard_map/all_to_all | solution.py:470
  102.6 2.2 %reduce_sum.37 = f32[2048]{0:T(1024)} reduce(f32[2048,128]{1,0:T(8,128)} %get-tuple-element.62, f32[]{:T(128)} %constant.16.clone.1), dimensions={1}, to_apply=%region_1.0 | reduce | flops 260096 | bytes 1056772 | tf_op jit(solution)/shard_map/reduce_sum | solution.py:573
  104.8 6.6 %outs.1 = (bf16[128,4096]{1,0:T(8,128)(2,1)}, bf16[128,4096]{1,0:T(8,128)(2,1)}, bf16[128,4096]{1,0:T(8,128)(2,1)}, f32[6,32,128]{2,1,0:T(8,128)S(1)}) custom-call(f32[4,4096]{1,0:T(4,128)} %w_ref.3, f32[4096,128]{1,0:T(8,128)} %get-tuple-element.56.dcv_hbm, f32[4096,128]{1,0:T(8,128)} %get-tuple-element.57.gz_hbm, f32[4096,128]{1,0:T(8,128)} %get-tuple-element.58.dd_hbm), custom_call_target="tpu_custom_call" | custom-call | flops 4194304 | bytes 10485760 | tf_op jit(solution)/shard_map/outs/pallas_call | solution.py:557
  111.4 3.4 %all-to-all-done.2 = f32[16,48,128]{2,1,0:T(8,128)S(1)} async-done(((f32[16,48,128]{2,1,0:T(8,128)}), f32[16,48,128]{2,1,0:T(8,128)S(1)}, u32[]{:S(2)}, u32[]{:S(2)}) %all-to-all-start.2) | async-done | bytes 393248 | tf_op jit(solution)/shard_map/all_to_all | solution.py:470
  114.9 0.8 broadcast_in_dim.2
  115.7 3.6 %all-to-all-start.3 = ((f32[16,48,128]{2,1,0:T(8,128)}), f32[16,48,128]{2,1,0:T(8,128)S(1)}, u32[]{:S(2)}, u32[]{:S(2)}) async-start(f32[16,48,128]{2,1,0:T(8,128)} %broadcast_in_dim.2), calls=%async_computation.3 | async-start | bytes 786432 | tf_op jit(solution)/shard_map/all_to_all | solution.py:470
  119.3 1.3 collective-permute-start.1
  120.6 4.6 %reduce_sum.39 = f32[16384]{0:T(1024)S(1)} reduce(f32[16384,128]{1,0:T(8,128)} %get-tuple-element.66, f32[]{:T(128)} %constant.16.clone.1), dimensions={1}, to_apply=%region_2.0 | reduce | flops 2080768 | bytes 8454148 | tf_op jit(solution)/shard_map/reduce_sum | solution.py:575
  125.2 0.6 reduce_sum.40
  125.8 0.9 reduce_sum.41
  126.7 0.0 collective-permute-done.1
  126.8 1.5 %dynamic_update_slice.3 = bf16[128,4096]{1,0:T(8,128)(2,1)} dynamic-update-slice(bf16[128,4096]{1,0:T(8,128)(2,1)} %get-tuple-element.59, bf16[3,4096]{1,0:T(4,128)(2,1)S(1)} %bitcast.28, s32[]{:T(128)} %constant.17.clone.1, s32[]{:T(128)} %constant.7.clone.1) | dynamic-update-slice | bytes 49156 | tf_op jit(solution)/shard_map/dynamic_update_slice | solution.py:578
  128.3 3.1 %all-to-all-done.3 = f32[16,48,128]{2,1,0:T(8,128)S(1)} async-done(((f32[16,48,128]{2,1,0:T(8,128)}), f32[16,48,128]{2,1,0:T(8,128)S(1)}, u32[]{:S(2)}, u32[]{:S(2)}) %all-to-all-start.3) | async-done | bytes 393248 | tf_op jit(solution)/shard_map/all_to_all | solution.py:470
  131.4 0.8 finish.1
  (5 shorter events, 0.1 us)
Async XLA Ops:
  1.5 9.1 %collective-permute-start = (bf16[3,32,128]{2,1,0:T(8,128)(2,1)S(1)}, bf16[3,32,128]{2,1,0:T(8,128)(2,1)S(1)}, u32[]{:S(2)}, u32[]{:S(2)}) collective-permute-start(bf16[3,32,128]{2,1,0:T(8,128)(2,1)S(1)} %bitcast.29), channel_id=1, source_target_pairs={{0,2},{2,4},{4,6},{6,8},{8,10},{10,12},{12,14},{14,16},{16,18},{18... | collective-permute-start | bytes 73736 | tf_op jit(solution)/shard_map/ppermute | solution.py:495
  23.5 41.7 %copy-start = (f32[4192,128]{1,0:T(8,128)}, f32[4192,128]{1,0:T(8,128)S(1)}, u32[]{:S(2)}) copy-start(f32[4192,128]{1,0:T(8,128)S(1)} %get-tuple-element.55.xs) | copy-start | bytes 6438916
  98.5 16.3 %all-to-all-start.2 = ((f32[16,48,128]{2,1,0:T(8,128)}), f32[16,48,128]{2,1,0:T(8,128)S(1)}, u32[]{:S(2)}, u32[]{:S(2)}) async-start(f32[16,48,128]{2,1,0:T(8,128)} %bitcast.7), calls=%async_computation.2 | async-start | bytes 786432 | tf_op jit(solution)/shard_map/all_to_all | solution.py:470
  115.7 15.7 %all-to-all-start.3 = ((f32[16,48,128]{2,1,0:T(8,128)}), f32[16,48,128]{2,1,0:T(8,128)S(1)}, u32[]{:S(2)}, u32[]{:S(2)}) async-start(f32[16,48,128]{2,1,0:T(8,128)} %broadcast_in_dim.2), calls=%async_computation.3 | async-start | bytes 786432 | tf_op jit(solution)/shard_map/all_to_all | solution.py:470
  119.3 7.5 %collective-permute-start.1 = (f32[3,32,128]{2,1,0:T(8,128)S(1)}, f32[3,32,128]{2,1,0:T(8,128)S(1)}, u32[]{:S(2)}, u32[]{:S(2)}) collective-permute-start(f32[3,32,128]{2,1,0:T(8,128)S(1)} %slice.11), channel_id=1, source_target_pairs={{2,0},{4,2},{6,4},{8,6},{10,8},{12,10},{14,12},{16,14},{18,16},{20... | collective-permute-start | bytes 147464 | tf_op jit(solution)/shard_map/ppermute | solution.py:576

commit v5 on v4

--- a/solution.py
+++ b/solution.py
@@ -257,7 +257,7 @@
 def grads_body(
     tokens, blocks, nstate, taps,
     in_ref, skip_ref, skipped_ref, dts, dus, gys, us, zfs, sls, sds, xs, bs, cs, nrates,
-    dcv_hbm, gz_hbm, dd_hbm, gb_hbm, gc_ref, par_ref,
+    dcv_hbm, gz_hbm, dd_hbm, gb_hbm, gc_hbm, par_ref,
     ys, gbs, dds, hs, pcs, pbs, sems, sum_sems,
 ):
     lead = taps - 1
@@ -277,9 +277,9 @@
     cells = GROUP * parts
     share = GROUP * tokens * SUB
 
-    def leave(group):
+    def leave(group, src, dst, which):
         here = pl.ds(pl.multiple_of(group * share, SUB), share)
-        return pltpu.make_async_copy(pbs.at[here, :], gb_hbm.at[here, :], sum_sems.at[group])
+        return pltpu.make_async_copy(src.at[here, :], dst.at[here, :], sum_sems.at[which, group])
 
     def some(group, carry):
         first = group * GROUP
@@ -317,13 +317,13 @@
                     y[m] = y[m] + cc * now
                     term = gy[m] * now
                     pulled = term if pulled is None else pulled + term
-                pcs[tile((n * tokens + t) * SUB), :] = pulled
+                pcs[tile(((first + n) * tokens + t) * SUB), :] = pulled
             for m in range(parts):
                 ys[tile(m * plane + t * SUB), :] = y[m]
             return tuple(state)
 
         steps(tokens, 64, forward, state)
-        fold(pcs, gc_ref, first * tokens, GROUP * tokens)
+        leave(group, pcs, gc_hbm, 0).start()
 
         def backward(step, carry):
             t = tokens - 1 - step
@@ -359,7 +359,7 @@
                 base = m * SUB * width + first + n
                 par_ref[pl.ds(base, SUB, stride=width), :] = acc[n * parts + m] / -rates[n * parts + m]
 
-        leave(group).start()
+        leave(group, pbs, gb_hbm, 1).start()
         return carry
 
     lax.fori_loop(0, nstate // GROUP, some, 0)
@@ -396,14 +396,15 @@
     for copy in copies:
         copy.wait()
     for group in range(nstate // GROUP):
-        leave(group).wait()
+        leave(group, pcs, gc_hbm, 0).wait()
+        leave(group, pbs, gb_hbm, 1).wait()
 
 
 def outs_body(
     tokens, blocks, taps,
-    w_ref, dcv_hbm, gz_hbm, dd_hbm,
-    gx_ref, gz_ref, gd_ref, owed_ref,
-    gbs, gzs, dds, ys, ws, sems,
+    w_ref, dcv_hbm, gz_hbm, dd_hbm, sum_hbm,
+    gx_ref, gz_ref, gd_ref, gc_ref, owed_ref,
+    gbs, gzs, dds, pcs, ys, ws, sems,
 ):
     lead = taps - 1
     parts = blocks // SUB
@@ -411,7 +412,9 @@
     zero = jnp.zeros((SUB, LANE), jnp.float32)
     copies = [
         pltpu.make_async_copy(src, dst, sems.at[i])
-        for i, (src, dst) in enumerate(((dcv_hbm, gbs), (gz_hbm, gzs), (dd_hbm, dds)))
+        for i, (src, dst) in enumerate(
+            ((dcv_hbm, gbs), (gz_hbm, gzs), (dd_hbm, dds), (sum_hbm, pcs))
+        )
     ]
     for copy in copies:
         copy.start()
@@ -449,6 +452,8 @@
     copies[1].wait()
     copies[2].wait()
     gather_tokens(((ys, gx_ref), (gzs, gz_ref), (dds, gd_ref)))
+    copies[3].wait()
+    fold(pcs, gc_ref, 0, gc_ref.shape[0])
 
 
 def slices(rows, runs):
@@ -541,38 +546,41 @@
     away = lambda rows: pltpu.HBM((rows, LANE), jnp.float32)
     dcv, gz, dd, gb, gc, par = pl.pallas_call(
         functools.partial(grads_body, tokens, blocks, nstate, taps),
-        out_shape=(*[away(full)] * 3, away(splats * SUB), away(splats), f32(blocks * rows, LANE)),
+        out_shape=(*[away(full)] * 3, *[away(splats * SUB)] * 2, f32(blocks * rows, LANE)),
         in_specs=[vmem] * 14,
-        out_specs=(*[hbm] * 4, vmem, vmem),
+        out_specs=(*[hbm] * 5, vmem),
         scratch_shapes=[
             vec(full), vec(full), vec(full), vec((tokens + 1) * GROUP * blocks),
-            vec(GROUP * tokens * SUB), vec(splats * SUB), pltpu.SemaphoreType.DMA((blocks // SUB, 3)),
-            pltpu.SemaphoreType.DMA((nstate // GROUP,)),
+            vec(splats * SUB), vec(splats * SUB), pltpu.SemaphoreType.DMA((blocks // SUB, 3)),
+            pltpu.SemaphoreType.DMA((2, nstate // GROUP)),
         ],
         compiler_params=limit(GRADS_MB),
         cost_estimate=cost(22, nstate * full * LANE),
         name="grads",
     )(ins.reshape(blocks * 2 * nstate, LANE), *far(skip), skipped, *factors)
     summed = swap(slices(par.reshape(blocks, rows, LANE), runs))
-    gx, gz, gd, owed = pl.pallas_call(
+    gx, gz, gd, gc, owed = pl.pallas_call(
         functools.partial(outs_body, tokens, blocks, taps),
-        out_shape=(*[pltpu.HBM((tokens, channels), jnp.bfloat16)] * 3, f32(2 * lead, blocks, LANE)),
-        in_specs=[vmem] + [hbm] * 3,
-        out_specs=tuple([vmem] * 4),
+        out_shape=(
+            *[pltpu.HBM((tokens, channels), jnp.bfloat16)] * 3, away(splats),
+            f32(2 * lead, blocks, LANE),
+        ),
+        in_specs=[vmem] + [hbm] * 4,
+        out_specs=tuple([vmem] * 5),
         scratch_shapes=[
-            vec(full), vec(full), vec(full), vec(full), vec(taps * blocks),
-            pltpu.SemaphoreType.DMA((3,)),
+            vec(full), vec(full), vec(full), vec(splats * SUB), vec(full), vec(taps * blocks),
+            pltpu.SemaphoreType.DMA((4,)),
         ],
         compiler_params=limit(GRADS_MB),
         cost_estimate=pl.CostEstimate(
             flops=8 * full * LANE, bytes_accessed=5 * full * LANE * 4, transcendentals=0
         ),
         name="outs",
-    )(*far(conv_w, dcv, gz, dd))
+    )(*far(conv_w, dcv, gz, dd, gc))
     sums = jnp.sum(summed, axis=0)
+    sums, owed = lax.optimization_barrier((sums, owed))
+    gb = jnp.sum(gb.reshape(nstate, tokens, SUB, LANE), axis=(2, 3))
     gc = jnp.sum(gc.reshape(nstate, tokens, LANE), axis=2)
-    sums, owed, gc = lax.optimization_barrier((sums, owed, gc))
-    gb = jnp.sum(gb.reshape(nstate, tokens, SUB, LANE), axis=(2, 3))
     returned = lax.ppermute(owed[:lead], "seq", [(i + 1, i) for i in range(runs - 1)])
     last = (owed[lead:] + returned).reshape(lead, channels).astype(jnp.bfloat16)
     gx = lax.dynamic_update_slice(gx, last, (tokens - lead, 0))

time: 133 us -> 131 us (0.985)
  waiting for transfers between devices: 6.52 us -> 4.88 us
    pallas_call x1, Pallas kernels: 6.62 us -> 9.47 us  [shards(): pl.pallas_call(functools.partial(outs_body, tokens, blocks, taps), out_sh...]
    all_to_all x2, waiting for transfers between devices: 6.52 us -> 4.88 us  [swap(): return lax.all_to_all(pieces, 'seq', 0, 0, tiled=True)]
    pallas_call x1, Pallas kernels: 33.4 us -> 31.9 us  [shards(): pl.pallas_call(functools.partial(grads_body, tokens, blocks, nstate, taps...]
  transfers between devices with their start and end apart: 4 -> 4, of which waited for: 2 -> 2; matrix products, arithmetic and copies ran while one was open for 8% -> 7% of each run, Pallas kernels for 10% -> 12%
where the time goes in v5:
time: 131 us
  Pallas kernels  61 us (47%)
  blocking collectives  41.6 us (32%)
  starting transfers between devices  11.3 us (9%)
  other arithmetic  6.56 us (5%)
  waiting for transfers between devices  4.88 us (4%)
  local copies, waits for them, and re-layouts  4.54 us (3%)
    all_to_all x2, blocking collectives, swap(): return lax.all_to_all(pieces, 'seq', 0, 0, tiled=True)  41.6 us
    pallas_call x1, Pallas kernels, shards(): pl.pallas_call(functools.partial(grads_body, tokens, blocks, nstate, taps...  31.9 us
    pallas_call x1, Pallas kernels, shards(): pl.pallas_call(functools.partial(local_body, tokens, blocks, nstate, taps...  12.8 us
    pallas_call x1, Pallas kernels, shards(): pl.pallas_call(functools.partial(outs_body, tokens, blocks, taps), out_sh...  9.47 us
    all_to_all x2, starting transfers between devices, swap(): return lax.all_to_all(pieces, 'seq', 0, 0, tiled=True)  7.66 us
    pallas_call x1, Pallas kernels, shards(): pl.pallas_call(functools.partial(prepare_body, tokens, blocks, nstate, ta...  5.97 us
    reduce_sum x2, other arithmetic, shards(): gb = jnp.sum(gb.reshape(nstate, tokens, SUB, LANE), axis=(2, 3))  5.57 us
    all_to_all x2, waiting for transfers between devices, swap(): return lax.all_to_all(pieces, 'seq', 0, 0, tiled=True)  4.88 us
  transfers between devices with their start and end apart: 4, of which 2 were waited for; matrix products, arithmetic and copies ran while one was open for 7% of the time, Pallas kernels for 12%

profile of v5, /device:TPU:0, one launch (start us, length us, event | category | flops | bytes accessed | tf_op | source)
XLA Modules:
  0.0 130.6 jit_solution(17499414061962315918)
XLA Ops:
  0.6 0.9 slice_bitcast_fusion
  1.5 2.4 %collective-permute-start = (bf16[3,32,128]{2,1,0:T(8,128)(2,1)S(1)}, bf16[3,32,128]{2,1,0:T(8,128)(2,1)S(1)}, u32[]{:S(2)}, u32[]{:S(2)}) collective-permute-start(bf16[3,32,128]{2,1,0:T(8,128)(2,1)S(1)} %bitcast.29), channel_id=1, source_target_pairs={{0,2},{2,4},{4,6},{6,8},{8,10},{10,12},{12,14},{14,16},{16,18},{18... | collective-permute-start | bytes 73736 | tf_op jit(solution)/shard_map/ppermute | solution.py:500
  3.9 0.7 constant_dynamic-slice_fusion.rate_mine_ref.rate_ref
  4.6 6.0 %prepare.1 = (f32[4096,128]{1,0:T(8,128)S(1)}, f32[4096,128]{1,0:T(8,128)S(1)}, f32[4096,128]{1,0:T(8,128)S(1)}, f32[4096,128]{1,0:T(8,128)S(1)}, f32[4192,128]{...) custom-call(bf16[128,4096]{1,0:T(8,128)(2,1)} %x_hbm.1, ...), custom_call_target="tpu_custom_call" | custom-call | flops 25165824 | bytes 4194304 | tf_op jit(solution)/shard_map/prepare/pallas_call | solution.py:507
  10.6 0.0 collective-permute-done.rim_ref
  10.6 12.8 %local_scan.1 = (f32[1152,128]{1,0:T(8,128)S(1)}, f32[32,128]{1,0:T(8,128)S(1)}, f32[4096,128]{1,0:T(8,128)S(1)}, f32[4096,128]{1,0:T(8,128)S(1)}, f32[4096,128]{1,0:T(8,128)S(1)}, /*index=5*/f32[4192,128]{1,0:T(8,128)S(1)}) custom-call(bf16[3,32,128]{2,1,0:T(8,128)(2,1)S(1)} %collective-permute-done.rim_ref, ...), custom_call_target="tpu_custom_call", output_to_operand_aliasing={{5}: (8, {})} | custom-call | flops 75497472 | bytes 18874368 | tf_op jit(solution)/shard_map/local_scan/pallas_call | solution.py:521
  23.5 0.0 copy-start
  23.5 24.3 %all_to_all.20 = f32[16,72,128]{2,1,0:T(8,128)S(1)} all-to-all(f32[16,72,128]{2,1,0:T(8,128)S(1)} %bitcast.27), channel_id=1, replica_groups=mesh['seq'=16,'dp'=2] {'seq'}, dimensions={0} | all-to-all | bytes 1179648 | tf_op jit(solution)/shard_map/all_to_all | solution.py:475
  47.8 0.1 carry_scan.1
  47.9 17.3 %all_to_all.21 = f32[16,64,128]{2,1,0:T(8,128)S(1)} all-to-all(f32[16,64,128]{2,1,0:T(8,128)S(1)} %bitcast.25), channel_id=1, replica_groups=mesh['seq'=16,'dp'=2] {'seq'}, dimensions={0} | all-to-all | bytes 1048576 | tf_op jit(solution)/shard_map/all_to_all | solution.py:475
  65.1 0.0 copy-done
  65.1 31.9 %grads.1 = (f32[4096,128]{1,0:T(8,128)}, f32[4096,128]{1,0:T(8,128)}, f32[4096,128]{1,0:T(8,128)}, f32[16384,128]{1,0:T(8,128)}, f32[16384,128]{1,0:T(8,128)}, /*index=5*/f32[768,128]{1,0:T(8,128)}) custom-call(f32[1024,128]{1,0:T(8,128)S(1)} %bitcast.24, f32[32,128]{1,0:T(8,128)} %bitcast.30, f32[32,128]{1,0:T(8,128)S(1)} %get-tuple-element.49.skipped_ref, ...), custom_call_target="tpu_custom_call" | custom-call | flops 184549376 | bytes 8388608 | tf_op jit(solution)/shard_map/grads/pallas_call | solution.py:547
  97.0 4.1 %all-to-all-start.2 = ((f32[16,48,128]{2,1,0:T(8,128)}), f32[16,48,128]{2,1,0:T(8,128)S(1)}, u32[]{:S(2)}, u32[]{:S(2)}) async-start(f32[16,48,128]{2,1,0:T(8,128)} %bitcast.7), calls=%async_computation.2 | async-start | bytes 786432 | tf_op jit(solution)/shard_map/all_to_all | solution.py:475
  101.1 9.5 %outs.1 = (bf16[128,4096]{1,0:T(8,128)(2,1)}, bf16[128,4096]{1,0:T(8,128)(2,1)}, bf16[128,4096]{1,0:T(8,128)(2,1)}, f32[2048,128]{1,0:T(8,128)}, f32[6,32,128]{2,1,0:T(8,128)S(1)}) custom-call(f32[4,4096]{1,0:T(4,128)} %w_ref.3, f32[4096,128]{1,0:T(8,128)} %get-tuple-element.56.dcv_hbm, f32[4096,128]{1,0:T(8,128)} %get-tuple-element.57.gz_hbm, ...), custom_call_target="tpu_custom_call" | custom-call | flops 4194304 | bytes 10485760 | tf_op jit(solution)/shard_map/outs/pallas_call | solution.py:562
  110.6 0.0 copy-start.1
  110.6 2.7 %all-to-all-done.2 = f32[16,48,128]{2,1,0:T(8,128)S(1)} async-done(((f32[16,48,128]{2,1,0:T(8,128)}), f32[16,48,128]{2,1,0:T(8,128)S(1)}, u32[]{:S(2)}, u32[]{:S(2)}) %all-to-all-start.2) | async-done | bytes 393248 | tf_op jit(solution)/shard_map/all_to_all | solution.py:475
  113.3 0.8 broadcast_in_dim.2
  114.2 3.6 %all-to-all-start.3 = ((f32[16,48,128]{2,1,0:T(8,128)}), f32[16,48,128]{2,1,0:T(8,128)S(1)}, u32[]{:S(2)}, u32[]{:S(2)}) async-start(f32[16,48,128]{2,1,0:T(8,128)} %broadcast_in_dim.2), calls=%async_computation.3 | async-start | bytes 786432 | tf_op jit(solution)/shard_map/all_to_all | solution.py:475
  117.7 1.3 collective-permute-start.1
  119.0 0.0 copy-done.1
  119.0 0.9 reduce_sum.40
  120.0 4.6 %reduce_sum.37 = f32[16384]{0:T(1024)S(1)} reduce(f32[16384,128]{1,0:T(8,128)} %get-tuple-element.66, f32[]{:T(128)} %constant.16.clone.1), dimensions={1}, to_apply=%region_1.0 | reduce | flops 2080768 | bytes 8454148 | tf_op jit(solution)/shard_map/reduce_sum | solution.py:582
  124.6 0.6 reduce_sum.38
  125.2 0.9 reduce_sum.39
  126.1 0.0 collective-permute-done.1
  126.2 1.5 %dynamic_update_slice.3 = bf16[128,4096]{1,0:T(8,128)(2,1)} dynamic-update-slice(bf16[128,4096]{1,0:T(8,128)(2,1)} %get-tuple-element.60, bf16[3,4096]{1,0:T(4,128)(2,1)S(1)} %bitcast.28, s32[]{:T(128)} %constant.17.clone.1, s32[]{:T(128)} %constant.7.clone.1) | dynamic-update-slice | bytes 49156 | tf_op jit(solution)/shard_map/dynamic_update_slice | solution.py:586
  127.7 2.2 %all-to-all-done.3 = f32[16,48,128]{2,1,0:T(8,128)S(1)} async-done(((f32[16,48,128]{2,1,0:T(8,128)}), f32[16,48,128]{2,1,0:T(8,128)S(1)}, u32[]{:S(2)}, u32[]{:S(2)}) %all-to-all-start.3) | async-done | bytes 393248 | tf_op jit(solution)/shard_map/all_to_all | solution.py:475
  129.9 0.8 finish.1
  (5 shorter events, 0.1 us)
Async XLA Ops:
  1.5 9.1 %collective-permute-start = (bf16[3,32,128]{2,1,0:T(8,128)(2,1)S(1)}, bf16[3,32,128]{2,1,0:T(8,128)(2,1)S(1)}, u32[]{:S(2)}, u32[]{:S(2)}) collective-permute-start(bf16[3,32,128]{2,1,0:T(8,128)(2,1)S(1)} %bitcast.29), channel_id=1, source_target_pairs={{0,2},{2,4},{4,6},{6,8},{8,10},{10,12},{12,14},{14,16},{16,18},{18... | collective-permute-start | bytes 73736 | tf_op jit(solution)/shard_map/ppermute | solution.py:500
  23.5 41.7 %copy-start = (f32[4192,128]{1,0:T(8,128)}, f32[4192,128]{1,0:T(8,128)S(1)}, u32[]{:S(2)}) copy-start(f32[4192,128]{1,0:T(8,128)S(1)} %get-tuple-element.55.xs) | copy-start | bytes 6438916
  97.0 16.3 %all-to-all-start.2 = ((f32[16,48,128]{2,1,0:T(8,128)}), f32[16,48,128]{2,1,0:T(8,128)S(1)}, u32[]{:S(2)}, u32[]{:S(2)}) async-start(f32[16,48,128]{2,1,0:T(8,128)} %bitcast.7), calls=%async_computation.2 | async-start | bytes 786432 | tf_op jit(solution)/shard_map/all_to_all | solution.py:475
  110.6 8.4 %copy-start.1 = (f32[2048,128]{1,0:T(8,128)S(1)}, f32[2048,128]{1,0:T(8,128)}, u32[]{:S(2)}) copy-start(f32[2048,128]{1,0:T(8,128)} %get-tuple-element.67) | copy-start | bytes 3145732
  114.2 15.7 %all-to-all-start.3 = ((f32[16,48,128]{2,1,0:T(8,128)}), f32[16,48,128]{2,1,0:T(8,128)S(1)}, u32[]{:S(2)}, u32[]{:S(2)}) async-start(f32[16,48,128]{2,1,0:T(8,128)} %broadcast_in_dim.2), calls=%async_computation.3 | async-start | bytes 786432 | tf_op jit(solution)/shard_map/all_to_all | solution.py:475
  117.7 8.4 %collective-permute-start.1 = (f32[3,32,128]{2,1,0:T(8,128)S(1)}, f32[3,32,128]{2,1,0:T(8,128)S(1)}, u32[]{:S(2)}, u32[]{:S(2)}) collective-permute-start(f32[3,32,128]{2,1,0:T(8,128)S(1)} %slice.11), channel_id=1, source_target_pairs={{2,0},{4,2},{6,4},{8,6},{10,8},{12,10},{14,12},{16,14},{18,16},{20... | collective-permute-start | bytes 147464 | tf_op jit(solution)/shard_map/ppermute | solution.py:584

commit v6 on v5

--- a/solution.py
+++ b/solution.py
@@ -145,7 +145,7 @@
             zfs[here, :] = gof * (1.0 + zf * (1.0 - sig_z))
             return carry
 
-        steps(tokens, 16, pre, 0)
+        steps(tokens, 32, pre, 0)
 
 
 def local_body(
@@ -177,7 +177,7 @@
             sls[here, :] = sig_c * (1.0 + conv * (1.0 - sig_c))
             return totals[0] + delta, totals[1] + gys[here, :] * inner
 
-        total, skipped = steps(tokens, 16, pre, (zero, zero))
+        total, skipped = steps(tokens, 32, pre, (zero, zero))
         pay_ref[pl.ds(m * SUB * width + 2 * nstate, SUB, stride=width), :] = total
         skip_ref[m * SUB : (m + 1) * SUB, :] = skipped
 
@@ -383,7 +383,7 @@
             )
             return bias + dd, convb + dcv, convw
 
-        bias, convb, convw = steps(tokens, 16, post, (zero, zero, (zero,) * taps))
+        bias, convb, convw = steps(tokens, 32, post, (zero, zero, (zero,) * taps))
         values = list(convw) + [convb, skipped_ref[m * SUB : (m + 1) * SUB, :], bias]
         for row, value in enumerate(values):
             par_ref[pl.ds(m * SUB * width + nstate + row, SUB, stride=width), :] = value

time: 131 us -> 131 us (level)
  no operation moved by 1% of the time
where the time goes in v6:
time: 131 us; the launch traced here: 130 us
  Pallas kernels  60.5 us (46%)
  blocking collectives  41.6 us (32%)
  starting transfers between devices  11.3 us (9%)
  other arithmetic  6.56 us (5%)
  waiting for transfers between devices  4.88 us (4%)
  local copies, waits for them, and re-layouts  4.54 us (3%)
    all_to_all x2, blocking collectives, swap(): return lax.all_to_all(pieces, 'seq', 0, 0, tiled=True)  41.6 us
    pallas_call x1, Pallas kernels, shards(): pl.pallas_call(functools.partial(grads_body, tokens, blocks, nstate, taps...  31.8 us
    pallas_call x1, Pallas kernels, shards(): pl.pallas_call(functools.partial(local_body, tokens, blocks, nstate, taps...  12.6 us
    pallas_call x1, Pallas kernels, shards(): pl.pallas_call(functools.partial(outs_body, tokens, blocks, taps), out_sh...  9.47 us
    all_to_all x2, starting transfers between devices, swap(): return lax.all_to_all(pieces, 'seq', 0, 0, tiled=True)  7.66 us
    pallas_call x1, Pallas kernels, shards(): pl.pallas_call(functools.partial(prepare_body, tokens, blocks, nstate, ta...  5.77 us
    reduce_sum x2, other arithmetic, shards(): gb = jnp.sum(gb.reshape(nstate, tokens, SUB, LANE), axis=(2, 3))  5.57 us
    all_to_all x2, waiting for transfers between devices, swap(): return lax.all_to_all(pieces, 'seq', 0, 0, tiled=True)  4.88 us
  transfers between devices with their start and end apart: 4, of which 2 were waited for; matrix products, arithmetic and copies ran while one was open for 7% of the time, Pallas kernels for 12%

profile of v6, /device:TPU:0, one launch (start us, length us, event | category | flops | bytes accessed | tf_op | source)
XLA Modules:
  0.0 130.2 jit_solution(1342992101297837815)
XLA Ops:
  0.6 0.9 slice_bitcast_fusion
  1.5 2.4 %collective-permute-start = (bf16[3,32,128]{2,1,0:T(8,128)(2,1)S(1)}, bf16[3,32,128]{2,1,0:T(8,128)(2,1)S(1)}, u32[]{:S(2)}, u32[]{:S(2)}) collective-permute-start(bf16[3,32,128]{2,1,0:T(8,128)(2,1)S(1)} %bitcast.29), channel_id=1, source_target_pairs={{0,2},{2,4},{4,6},{6,8},{8,10},{10,12},{12,14},{14,16},{16,18},{18... | collective-permute-start | bytes 73736 | tf_op jit(solution)/shard_map/ppermute | solution.py:500
  3.9 0.7 constant_dynamic-slice_fusion.rate_mine_ref.rate_ref
  4.6 5.8 %prepare.1 = (f32[4096,128]{1,0:T(8,128)S(1)}, f32[4096,128]{1,0:T(8,128)S(1)}, f32[4096,128]{1,0:T(8,128)S(1)}, f32[4096,128]{1,0:T(8,128)S(1)}, f32[4192,128]{...) custom-call(bf16[128,4096]{1,0:T(8,128)(2,1)} %x_hbm.1, ...), custom_call_target="tpu_custom_call" | custom-call | flops 25165824 | bytes 4194304 | tf_op jit(solution)/shard_map/prepare/pallas_call | solution.py:507
  10.4 0.0 collective-permute-done.rim_ref
  10.4 12.6 %local_scan.1 = (f32[1152,128]{1,0:T(8,128)S(1)}, f32[32,128]{1,0:T(8,128)S(1)}, f32[4096,128]{1,0:T(8,128)S(1)}, f32[4096,128]{1,0:T(8,128)S(1)}, f32[4096,128]{1,0:T(8,128)S(1)}, /*index=5*/f32[4192,128]{1,0:T(8,128)S(1)}) custom-call(bf16[3,32,128]{2,1,0:T(8,128)(2,1)S(1)} %collective-permute-done.rim_ref, ...), custom_call_target="tpu_custom_call", output_to_operand_aliasing={{5}: (8, {})} | custom-call | flops 75497472 | bytes 18874368 | tf_op jit(solution)/shard_map/local_scan/pallas_call | solution.py:521
  23.0 0.0 copy-start
  23.0 24.3 %all_to_all.20 = f32[16,72,128]{2,1,0:T(8,128)S(1)} all-to-all(f32[16,72,128]{2,1,0:T(8,128)S(1)} %bitcast.27), channel_id=1, replica_groups=mesh['seq'=16,'dp'=2] {'seq'}, dimensions={0} | all-to-all | bytes 1179648 | tf_op jit(solution)/shard_map/all_to_all | solution.py:475
  47.3 0.1 carry_scan.1
  47.4 17.3 %all_to_all.21 = f32[16,64,128]{2,1,0:T(8,128)S(1)} all-to-all(f32[16,64,128]{2,1,0:T(8,128)S(1)} %bitcast.25), channel_id=1, replica_groups=mesh['seq'=16,'dp'=2] {'seq'}, dimensions={0} | all-to-all | bytes 1048576 | tf_op jit(solution)/shard_map/all_to_all | solution.py:475
  64.7 0.0 copy-done
  64.7 31.8 %grads.1 = (f32[4096,128]{1,0:T(8,128)}, f32[4096,128]{1,0:T(8,128)}, f32[4096,128]{1,0:T(8,128)}, f32[16384,128]{1,0:T(8,128)}, f32[16384,128]{1,0:T(8,128)}, /*index=5*/f32[768,128]{1,0:T(8,128)}) custom-call(f32[1024,128]{1,0:T(8,128)S(1)} %bitcast.24, f32[32,128]{1,0:T(8,128)} %bitcast.30, f32[32,128]{1,0:T(8,128)S(1)} %get-tuple-element.49.skipped_ref, ...), custom_call_target="tpu_custom_call" | custom-call | flops 184549376 | bytes 8388608 | tf_op jit(solution)/shard_map/grads/pallas_call | solution.py:547
  96.5 4.1 %all-to-all-start.2 = ((f32[16,48,128]{2,1,0:T(8,128)}), f32[16,48,128]{2,1,0:T(8,128)S(1)}, u32[]{:S(2)}, u32[]{:S(2)}) async-start(f32[16,48,128]{2,1,0:T(8,128)} %bitcast.7), calls=%async_computation.2 | async-start | bytes 786432 | tf_op jit(solution)/shard_map/all_to_all | solution.py:475
  100.7 9.5 %outs.1 = (bf16[128,4096]{1,0:T(8,128)(2,1)}, bf16[128,4096]{1,0:T(8,128)(2,1)}, bf16[128,4096]{1,0:T(8,128)(2,1)}, f32[2048,128]{1,0:T(8,128)}, f32[6,32,128]{2,1,0:T(8,128)S(1)}) custom-call(f32[4,4096]{1,0:T(4,128)} %w_ref.3, f32[4096,128]{1,0:T(8,128)} %get-tuple-element.56.dcv_hbm, f32[4096,128]{1,0:T(8,128)} %get-tuple-element.57.gz_hbm, ...), custom_call_target="tpu_custom_call" | custom-call | flops 4194304 | bytes 10485760 | tf_op jit(solution)/shard_map/outs/pallas_call | solution.py:562
  110.1 0.0 copy-start.1
  110.1 2.7 %all-to-all-done.2 = f32[16,48,128]{2,1,0:T(8,128)S(1)} async-done(((f32[16,48,128]{2,1,0:T(8,128)}), f32[16,48,128]{2,1,0:T(8,128)S(1)}, u32[]{:S(2)}, u32[]{:S(2)}) %all-to-all-start.2) | async-done | bytes 393248 | tf_op jit(solution)/shard_map/all_to_all | solution.py:475
  112.9 0.8 broadcast_in_dim.2
  113.7 3.6 %all-to-all-start.3 = ((f32[16,48,128]{2,1,0:T(8,128)}), f32[16,48,128]{2,1,0:T(8,128)S(1)}, u32[]{:S(2)}, u32[]{:S(2)}) async-start(f32[16,48,128]{2,1,0:T(8,128)} %broadcast_in_dim.2), calls=%async_computation.3 | async-start | bytes 786432 | tf_op jit(solution)/shard_map/all_to_all | solution.py:475
  117.3 1.3 collective-permute-start.1
  118.6 0.0 copy-done.1
  118.6 0.9 reduce_sum.40
  119.5 4.6 %reduce_sum.37 = f32[16384]{0:T(1024)S(1)} reduce(f32[16384,128]{1,0:T(8,128)} %get-tuple-element.66, f32[]{:T(128)} %constant.16.clone.1), dimensions={1}, to_apply=%region_1.0 | reduce | flops 2080768 | bytes 8454148 | tf_op jit(solution)/shard_map/reduce_sum | solution.py:582
  124.2 0.6 reduce_sum.38
  124.7 0.9 reduce_sum.39
  125.7 0.0 collective-permute-done.1
  125.7 1.5 %dynamic_update_slice.3 = bf16[128,4096]{1,0:T(8,128)(2,1)} dynamic-update-slice(bf16[128,4096]{1,0:T(8,128)(2,1)} %get-tuple-element.60, bf16[3,4096]{1,0:T(4,128)(2,1)S(1)} %bitcast.28, s32[]{:T(128)} %constant.17.clone.1, s32[]{:T(128)} %constant.7.clone.1) | dynamic-update-slice | bytes 49156 | tf_op jit(solution)/shard_map/dynamic_update_slice | solution.py:586
  127.3 2.2 %all-to-all-done.3 = f32[16,48,128]{2,1,0:T(8,128)S(1)} async-done(((f32[16,48,128]{2,1,0:T(8,128)}), f32[16,48,128]{2,1,0:T(8,128)S(1)}, u32[]{:S(2)}, u32[]{:S(2)}) %all-to-all-start.3) | async-done | bytes 393248 | tf_op jit(solution)/shard_map/all_to_all | solution.py:475
  129.4 0.8 finish.1
  (5 shorter events, 0.1 us)
Async XLA Ops:
  1.5 8.9 %collective-permute-start = (bf16[3,32,128]{2,1,0:T(8,128)(2,1)S(1)}, bf16[3,32,128]{2,1,0:T(8,128)(2,1)S(1)}, u32[]{:S(2)}, u32[]{:S(2)}) collective-permute-start(bf16[3,32,128]{2,1,0:T(8,128)(2,1)S(1)} %bitcast.29), channel_id=1, source_target_pairs={{0,2},{2,4},{4,6},{6,8},{8,10},{10,12},{12,14},{14,16},{16,18},{18... | collective-permute-start | bytes 73736 | tf_op jit(solution)/shard_map/ppermute | solution.py:500
  23.0 41.7 %copy-start = (f32[4192,128]{1,0:T(8,128)}, f32[4192,128]{1,0:T(8,128)S(1)}, u32[]{:S(2)}) copy-start(f32[4192,128]{1,0:T(8,128)S(1)} %get-tuple-element.55.xs) | copy-start | bytes 6438916
  96.5 16.3 %all-to-all-start.2 = ((f32[16,48,128]{2,1,0:T(8,128)}), f32[16,48,128]{2,1,0:T(8,128)S(1)}, u32[]{:S(2)}, u32[]{:S(2)}) async-start(f32[16,48,128]{2,1,0:T(8,128)} %bitcast.7), calls=%async_computation.2 | async-start | bytes 786432 | tf_op jit(solution)/shard_map/all_to_all | solution.py:475
  110.1 8.4 %copy-start.1 = (f32[2048,128]{1,0:T(8,128)S(1)}, f32[2048,128]{1,0:T(8,128)}, u32[]{:S(2)}) copy-start(f32[2048,128]{1,0:T(8,128)} %get-tuple-element.67) | copy-start | bytes 3145732
  113.7 15.7 %all-to-all-start.3 = ((f32[16,48,128]{2,1,0:T(8,128)}), f32[16,48,128]{2,1,0:T(8,128)S(1)}, u32[]{:S(2)}, u32[]{:S(2)}) async-start(f32[16,48,128]{2,1,0:T(8,128)} %broadcast_in_dim.2), calls=%async_computation.3 | async-start | bytes 786432 | tf_op jit(solution)/shard_map/all_to_all | solution.py:475
  117.3 8.4 %collective-permute-start.1 = (f32[3,32,128]{2,1,0:T(8,128)S(1)}, f32[3,32,128]{2,1,0:T(8,128)S(1)}, u32[]{:S(2)}, u32[]{:S(2)}) collective-permute-start(f32[3,32,128]{2,1,0:T(8,128)S(1)} %slice.11), channel_id=1, source_target_pairs={{2,0},{4,2},{6,4},{8,6},{10,8},{12,10},{14,12},{16,14},{18,16},{20... | collective-permute-start | bytes 147464 | tf_op jit(solution)/shard_map/ppermute | solution.py:584
